TPU v7x, 32 devices: a whole 2x2x4 slice. The times are simulated.
32 devices in a mesh: dp: 8 (over y, x, core), tensor: 4 (over z).
Axes of the slice: x: 2, y: 2, z: 4, core: 2. Of those that a mesh axis runs over, the one named last changes fastest.
Arguments:
- layer_input: bfloat16 [8192, 2048], P(('dp', 'tensor')), may hold values from -6 to 6
- output_grad: bfloat16 [8192, 2048], P(('dp', 'tensor')), may hold values from -6 to 6
- segment_ids: int32 [8, 1024], P('dp'), may hold values from 0 to 2, as said below
- norm_gain: float32 [2, 2048], replicated, may hold values from 0.5 to 1.5
- gain_mean: float32 [2, 2048], replicated, may hold values from -64 to 64
- gain_square: float32 [2, 2048], replicated, may hold values from 409.6 to 1638.4
- norm_shift: float32 [2, 2048], replicated, may hold values from -3 to 3
- shift_mean: float32 [2, 2048], replicated, may hold values from -64 to 64
- shift_square: float32 [2, 2048], replicated, may hold values from 409.6 to 1638.4
- qkv_bias: float32 [3, 2048], P(None, 'tensor'), may hold values from -3 to 3
- bias_mean: float32 [3, 2048], P(None, 'tensor'), may hold values from -128 to 128
- bias_square: float32 [3, 2048], P(None, 'tensor'), may hold values from 1638.4 to 6553.6
- qkv_weight: float32 [3, 2048, 2048], P(None, 'dp', 'tensor'), may hold values from -0.125 to 0.125
- qkv_mean: float32 [3, 2048, 2048], P(None, 'dp', 'tensor'), may hold values from -128 to 128
- qkv_square: float32 [3, 2048, 2048], P(None, 'dp', 'tensor'), may hold values from 1638.4 to 6553.6
- proj_weight: float32 [2048, 2048], P('tensor', 'dp'), may hold values from -0.5 to 0.5
- proj_mean: float32 [2048, 2048], P('tensor', 'dp'), may hold values from -24 to 24
- proj_square: float32 [2048, 2048], P('tensor', 'dp'), may hold values from 65.536 to 262.144
- feed_weight: float32 [2, 2048, 5632], P(None, 'dp', 'tensor'), may hold values from -0.125 to 0.125
- feed_mean: float32 [2, 2048, 5632], P(None, 'dp', 'tensor'), may hold values from -20 to 20
- feed_square: float32 [2, 2048, 5632], P(None, 'dp', 'tensor'), may hold values from 49.152 to 196.608
- down_weight: float32 [5632, 2048], P('tensor', 'dp'), may hold values from -0.078125 to 0.078125
- down_mean: float32 [5632, 2048], P('tensor', 'dp'), may hold values from -40 to 40
- down_square: float32 [5632, 2048], P('tensor', 'dp'), may hold values from 204.8 to 819.2
Outputs:
- layer_output: float32 [8192, 2048], P(('dp', 'tensor'))
- input_grad: float32 [8192, 2048], P(('dp', 'tensor'))
- gain_grad: float32 [2, 2048], replicated
- gain_step: float32 [2, 2048], replicated
- gain_newmean: float32 [2, 2048], replicated
- gain_newsquare: float32 [2, 2048], replicated
- shift_grad: float32 [2, 2048], replicated
- shift_step: float32 [2, 2048], replicated
- shift_newmean: float32 [2, 2048], replicated
- shift_newsquare: float32 [2, 2048], replicated
- bias_grad: float32 [3, 2048], P(None, 'tensor')
- bias_step: float32 [3, 2048], P(None, 'tensor')
- bias_newmean: float32 [3, 2048], P(None, 'tensor')
- bias_newsquare: float32 [3, 2048], P(None, 'tensor')
- qkv_grad: float32 [3, 2048, 2048], P(None, 'dp', 'tensor')
- qkv_updated: float32 [3, 2048, 2048], P(None, 'dp', 'tensor')
- qkv_newmean: float32 [3, 2048, 2048], P(None, 'dp', 'tensor')
- qkv_newsquare: float32 [3, 2048, 2048], P(None, 'dp', 'tensor')
- proj_grad: float32 [2048, 2048], P('tensor', 'dp')
- proj_updated: float32 [2048, 2048], P('tensor', 'dp')
- proj_newmean: float32 [2048, 2048], P('tensor', 'dp')
- proj_newsquare: float32 [2048, 2048], P('tensor', 'dp')
- feed_grad: float32 [2, 2048, 5632], P(None, 'dp', 'tensor')
- feed_updated: float32 [2, 2048, 5632], P(None, 'dp', 'tensor')
- feed_newmean: float32 [2, 2048, 5632], P(None, 'dp', 'tensor')
- feed_newsquare: float32 [2, 2048, 5632], P(None, 'dp', 'tensor')
- down_grad: float32 [5632, 2048], P('tensor', 'dp')
- down_updated: float32 [5632, 2048], P('tensor', 'dp')
- down_newmean: float32 [5632, 2048], P('tensor', 'dp')
- down_newsquare: float32 [5632, 2048], P('tensor', 'dp')
Inputs may be any that keep to these rules, and one draw needn't show every extreme that they name: `segment_ids`: in each packed sequence of 1024 tokens the segment numbers start at 0 and never fall; a number may be skipped; the last token's number is 2.
All inputs are finite; a program needn't handle non-finite values.
Results may differ from a plain program's by a relative error of at most 0.012.
Values may be sent and summed in bfloat16 or wider, within the bound.
No kernel may reach another device: no remote copies, remote signals or barrier semaphores. Data moves between devices by JAX's collectives and lax.ppermute only.
A program may use at most 256 MiB of HBM per device.

v0:
```python
import functools
import math

import jax
import jax.numpy as jnp
from jax import lax
from jax.experimental import pallas as pl
from jax.experimental.pallas import tpu as pltpu
from jax.sharding import PartitionSpec as P


HEAD = 64
ROT = 16
HALF = ROT // 2
STEP = 10
PAIR = 2
WIDE = 4
MASKED = -1000000000.0
BF16 = jnp.bfloat16
F32 = jnp.float32

norm_eps = 1e-05


def norm_forward(values, gain_row, shift_row):
    center = values - jnp.mean(values, axis=-1, keepdims=True)
    inverse = lax.rsqrt(jnp.mean(center * center, axis=-1, keepdims=True) + norm_eps)
    unit_rows = center * inverse
    return (unit_rows * gain_row + shift_row, unit_rows, inverse)


def norm_backward(grad_in, unit_rows, inverse, gain_row):
    scaled = grad_in * gain_row
    return inverse * (
        scaled
        - jnp.mean(scaled, axis=-1, keepdims=True)
        - unit_rows * jnp.mean(scaled * unit_rows, axis=-1, keepdims=True)
    )


def run_starts(segments):
    token_index = jnp.arange(segments.shape[1], dtype=jnp.int32)[None, :]
    starts = jnp.concatenate(
        [jnp.ones((1, 1), dtype=bool), segments[:, 1:] != segments[:, :-1]], axis=1
    )
    return lax.cummax(jnp.where(starts, token_index, 0), axis=1)


def rotary_tables(starts):
    token_index = jnp.arange(starts.shape[1], dtype=jnp.int32)[None, :]
    freqs = jnp.exp(jnp.arange(HALF, dtype=F32) * (-2.0 * math.log(10000.0) / ROT))
    angles = (token_index - starts).astype(F32) * freqs[:, None]
    return (jnp.cos(angles), jnp.sin(angles))


def adamw(param, grad_in, mean_in, square_in):
    mean_new = 0.9 * mean_in + 0.1 * grad_in
    square_new = 0.95 * square_in + 0.05 * grad_in * grad_in
    corrected = mean_new / (1.0 - 0.9**STEP)
    scaled = jnp.sqrt(square_new / (1.0 - 0.95**STEP)) + 1e-08
    change = -0.02 * (corrected / scaled + 0.1 * param)
    return (change, mean_new, square_new)


def contract(left, right, left_dim, right_dim):
    return lax.dot_general(
        left, right, (((left_dim,), (right_dim,)), ((), ())), preferred_element_type=F32
    )


def rope_kernel(where_ref, q_ref, k_ref, v_ref, cos_ref, sin_ref, old_ref, out_ref):
    del where_ref, old_ref
    cosine, sine = cos_ref[...], sin_ref[...]
    for which, ref in enumerate((q_ref, k_ref, v_ref)):
        whole = ref[...].T
        for head in range(WIDE):
            rows = slice(head * HEAD, (head + 1) * HEAD)
            part = whole[rows]
            if which < 2:
                first, second = part[:HALF], part[HALF:ROT]
                part = jnp.concatenate(
                    [
                        first * cosine - second * sine,
                        second * cosine + first * sine,
                        part[ROT:],
                    ],
                    axis=0,
                )
            if which == 0:
                part = part * (HEAD**-0.5)
            out_ref[which, rows, :] = part.astype(BF16)


def rope_block(where, pre, cosine, sine, buffer, width, length):
    rows = WIDE * HEAD
    groups = width // rows
    block = pre.shape[0]
    first = buffer is None
    body = rope_kernel
    specs = [
        pl.BlockSpec((block, rows), lambda h, s: (0, h)),
        pl.BlockSpec((block, rows), lambda h, s: (0, groups + h)),
        pl.BlockSpec((block, rows), lambda h, s: (0, 2 * groups + h)),
        pl.BlockSpec((HALF, block), lambda h, s: (0, s[0])),
        pl.BlockSpec((HALF, block), lambda h, s: (0, s[0])),
    ]
    args = [where, pre, pre, pre, cosine, sine]
    aliases = {}
    if first:
        body = lambda w, q, k, v, c, d, o: rope_kernel(w, q, k, v, c, d, None, o)
    else:
        specs.append(pl.BlockSpec(memory_space=pl.ANY))
        aliases = {len(args): 0}
        args.append(buffer)
    return pl.pallas_call(
        body,
        out_shape=jax.ShapeDtypeStruct((3, width, length), BF16),
        grid_spec=pltpu.PrefetchScalarGridSpec(
            num_scalar_prefetch=1,
            grid=(groups,),
            in_specs=specs,
            out_specs=pl.BlockSpec((3, rows, block), lambda h, s: (0, h, s[0])),
        ),
        input_output_aliases=aliases,
        cost_estimate=pl.CostEstimate(
            flops=6 * 3 * width * block, bytes_accessed=18 * width * block, transcendentals=0
        ),
        name="rope_block",
    )(*args)


def allowed(key_block, query_block, block, starts):
    shape = (block, block)
    key_at = lax.broadcasted_iota(jnp.int32, shape, 0) + key_block * block
    mask = key_at >= starts
    if key_block == query_block:
        query_at = lax.broadcasted_iota(jnp.int32, shape, 1) + query_block * block
        mask = mask & (key_at <= query_at)
    return mask


def attend_kernel(blocks, block, where_ref, starts_ref, q_ref, k_ref, v_ref, out_ref, total_ref):
    starts = starts_ref[...]
    for mine in range(blocks):

        @pl.when(where_ref[0] == mine)
        def _(mine=mine):
            for head in range(PAIR):
                rows = slice(head * HEAD, (head + 1) * HEAD)
                query = q_ref[0, rows, :]
                scores = []
                for other in range(mine + 1):
                    keys = k_ref[0, rows, other * block : (other + 1) * block]
                    raw = contract(keys, query, 0, 0)
                    scores.append(jnp.where(allowed(other, mine, block, starts), raw, MASKED))
                top = functools.reduce(
                    jnp.maximum, [jnp.max(s, axis=0, keepdims=True) for s in scores]
                )
                total = jnp.zeros((1, block), F32)
                result = jnp.zeros((HEAD, block), F32)
                for other, s in enumerate(scores):
                    terms = jnp.exp(s - top)
                    total = total + jnp.sum(terms, axis=0, keepdims=True)
                    values = v_ref[0, rows, other * block : (other + 1) * block]
                    result = result + contract(values, terms.astype(BF16), 1, 0)
                out_ref[rows, :] = (result / total).astype(BF16)
                total_ref[head] = top + jnp.log(total)


def attend_block(where, starts, buffer, block):
    _, width, length = buffer.shape
    rows = PAIR * HEAD
    heads, blocks = width // HEAD, length // block
    return pl.pallas_call(
        functools.partial(attend_kernel, blocks, block),
        out_shape=(
            jax.ShapeDtypeStruct((width, block), BF16),
            jax.ShapeDtypeStruct((heads, 1, block), F32),
        ),
        grid_spec=pltpu.PrefetchScalarGridSpec(
            num_scalar_prefetch=1,
            grid=(width // rows,),
            in_specs=[
                pl.BlockSpec((1, block), lambda h, s: (0, s[0])),
                pl.BlockSpec((1, rows, block), lambda h, s: (0, h, s[0])),
                pl.BlockSpec((1, rows, length), lambda h, s: (1, h, 0)),
                pl.BlockSpec((1, rows, length), lambda h, s: (2, h, 0)),
            ],
            out_specs=(
                pl.BlockSpec((rows, block), lambda h, s: (h, 0)),
                pl.BlockSpec((PAIR, 1, block), lambda h, s: (h, 0, 0)),
            ),
        ),
        cost_estimate=pl.CostEstimate(
            flops=16 * width * block * length,
            bytes_accessed=2 * width * (2 * length + 2 * block),
            transcendentals=heads * block * length,
        ),
        name="attend_block",
    )(where, starts, buffer, buffer, buffer)


def attend_back_kernel(blocks, block, first, last, where_ref, starts_ref, cos_ref, sin_ref, *refs):
    if last:
        all_cos_ref, all_sin_ref, *refs = refs
    q_ref, k_ref, v_ref, grad_ref, total_ref, *refs = refs
    if not first:
        old_out_ref, old_ref, *refs = refs
    if last:
        (out_ref,) = refs
    else:
        out_ref, sums_ref = refs
    starts = starts_ref[...]
    cosine, sine = cos_ref[...], sin_ref[...]

    def unrotate(part, cosine, sine):
        one, two = part[:HALF], part[HALF:ROT]
        return jnp.concatenate(
            [one * cosine + two * sine, two * cosine - one * sine, part[ROT:]], axis=0
        )

    def at_position(position):
        return pl.ds(pl.multiple_of(position * block, block), block)

    if last:
        for position in range(blocks):
            columns = slice(position * block, (position + 1) * block)
            out_ref[0, :, columns] = old_out_ref[:, columns]

    for mine in range(blocks):

        @pl.when(where_ref[0] == mine)
        def _(mine=mine):
            for head in range(PAIR):
                rows = slice(head * HEAD, (head + 1) * HEAD)
                query = q_ref[0, rows, :]
                grad = grad_ref[rows, :]
                row_total = total_ref[head]
                kept = []
                offset = jnp.zeros((1, block), F32)
                for other in range(mine + 1):
                    columns = slice(other * block, (other + 1) * block)
                    raw = contract(k_ref[0, rows, columns], query, 0, 0)
                    masked = jnp.where(allowed(other, mine, block, starts), raw, MASKED)
                    weights = jnp.exp(masked - row_total)
                    back = contract(v_ref[0, rows, columns], grad, 0, 0)
                    offset = offset + jnp.sum(weights * back, axis=0, keepdims=True)
                    kept.append((weights, back))
                query_sum = jnp.zeros((HEAD, block), F32)
                for other in range(blocks):
                    columns = slice(other * block, (other + 1) * block)
                    if other <= mine:
                        weights, back = kept[other]
                        change = (weights * (back - offset)).astype(BF16)
                        query_sum = query_sum + contract(k_ref[0, rows, columns], change, 1, 0)
                        key_sum = contract(query, change, 1, 1)
                        value_sum = contract(grad, weights.astype(BF16), 1, 1)
                        if not first:
                            key_sum = key_sum + old_ref[0, rows, columns]
                            value_sum = value_sum + old_ref[1, rows, columns]
                    elif first:
                        key_sum = jnp.zeros((HEAD, block), F32)
                        value_sum = jnp.zeros((HEAD, block), F32)
                    else:
                        key_sum = old_ref[0, rows, columns]
                        value_sum = old_ref[1, rows, columns]
                    if last:
                        there = at_position(lax.rem(where_ref[2] + blocks - other, blocks))
                        turned = unrotate(
                            key_sum, all_cos_ref[:, columns], all_sin_ref[:, columns]
                        )
                        out_ref[1, rows, there] = turned.astype(BF16)
                        out_ref[2, rows, there] = value_sum.astype(BF16)
                    else:
                        sums_ref[0, rows, columns] = key_sum
                        sums_ref[1, rows, columns] = value_sum
                query_sum = unrotate(query_sum * (HEAD**-0.5), cosine, sine).astype(BF16)
                if last:
                    out_ref[0, rows, at_position(where_ref[1])] = query_sum
                else:
                    out_ref[rows, :] = query_sum


def attend_back_block(where, starts, cosine, sine, buffer, grad, totals, before, last):
    _, width, length = buffer.shape
    block = grad.shape[1]
    rows = PAIR * HEAD
    heads, blocks = width // HEAD, length // block
    groups = width // rows
    first = before is None
    whole_table = pl.BlockSpec((HALF, length), lambda h, s: (0, 0))
    both = pl.BlockSpec((2, rows, length), lambda h, s: (0, h, 0))
    specs = [
        pl.BlockSpec((1, block), lambda h, s: (0, s[0])),
        pl.BlockSpec((HALF, block), lambda h, s: (0, s[0])),
        pl.BlockSpec((HALF, block), lambda h, s: (0, s[0])),
    ]
    args = [where, starts, cosine, sine]
    if last:
        specs += [whole_table, whole_table]
        args += [cosine, sine]
    specs += [
        pl.BlockSpec((1, rows, block), lambda h, s: (0, h, s[0])),
        pl.BlockSpec((1, rows, length), lambda h, s: (1, h, 0)),
        pl.BlockSpec((1, rows, length), lambda h, s: (2, h, 0)),
        pl.BlockSpec((rows, block), lambda h, s: (h, 0)),
        pl.BlockSpec((PAIR, 1, block), lambda h, s: (s[1] * groups + h, 0, 0)),
    ]
    args += [buffer, buffer, buffer, grad, totals]
    aliases = {}
    if not first:
        if last:
            specs += [pl.BlockSpec((rows, length), lambda h, s: (h, 0)), both]
        else:
            specs += [pl.BlockSpec(memory_space=pl.ANY), both]
            aliases = {len(args): 0, len(args) + 1: 1}
        args += before
    if last:
        out_shape = jax.ShapeDtypeStruct((3, width, length), BF16)
        out_specs = pl.BlockSpec((3, rows, length), lambda h, s: (0, h, 0))
    else:
        out_shape = (
            jax.ShapeDtypeStruct((width, length), BF16),
            jax.ShapeDtypeStruct((2, width, length), F32),
        )
        out_specs = (pl.BlockSpec((rows, block), lambda h, s: (h, s[1])), both)
    return pl.pallas_call(
        functools.partial(attend_back_kernel, blocks, block, first, last),
        out_shape=out_shape,
        grid_spec=pltpu.PrefetchScalarGridSpec(
            num_scalar_prefetch=1, grid=(groups,), in_specs=specs, out_specs=out_specs
        ),
        input_output_aliases=aliases,
        cost_estimate=pl.CostEstimate(
            flops=40 * width * block * length,
            bytes_accessed=2 * width * (10 * length + 3 * block),
            transcendentals=heads * block * length,
        ),
        name="attend_back_block",
    )(*args)


def per_device(
    ring_size,
    data_size,
    layer_input,
    output_grad,
    segment_ids,
    norm_gain,
    gain_mean,
    gain_square,
    norm_shift,
    shift_mean,
    shift_square,
    qkv_bias,
    bias_mean,
    bias_square,
    qkv_weight,
    qkv_mean,
    qkv_square,
    proj_weight,
    proj_mean,
    proj_square,
    feed_weight,
    feed_mean,
    feed_square,
    down_weight,
    down_mean,
    down_square,
):
    n = ring_size
    block, depth = layer_input.shape
    length = n * block
    width = qkv_bias.shape[1]
    units = feed_weight.shape[2]
    place = lax.axis_index("tensor")
    ring = [(i, (i + 1) % n) for i in range(n)]

    def after(value, *others):
        return lax.optimization_barrier((value, *others))[0]

    def pass_on(values, pairs=ring):
        return lax.ppermute(values, "tensor", pairs)

    def pass_up(values, first, last):
        return pass_on(values, [(i, i + 1) for i in range(first, last + 1)])

    def pass_down(values, first, last):
        return pass_on(values, [(i, i - 1) for i in range(first, last + 1)])

    def at_place(table):
        return jnp.asarray(table, jnp.int32)[place]

    def plus(term, moving):
        return (term + moving.astype(F32)).astype(BF16)

    arrivals = [
        sorted(
            [(d, 0) for d in range(1, z + 1)] + [(d, 1) for d in range(1, n - z)]
        )
        for z in range(n)
    ]

    def where_of(blocks_of_place):
        mine = at_place(blocks_of_place)
        return jnp.stack([mine, lax.rem(place + n - mine, n), place]).astype(jnp.int32)

    def gather_weight(shard, axis):
        return lax.all_gather(shard.astype(BF16), "dp", axis=axis, tiled=True)

    def apart(*values):
        return lax.optimization_barrier(values)

    inputs = layer_input.astype(F32)
    w_qkv = gather_weight(qkv_weight.transpose(0, 2, 1), 2).reshape(3 * width, depth)
    w_proj = gather_weight(proj_weight, 1)
    w_feed = gather_weight(feed_weight, 1)
    w_down = gather_weight(down_weight, 1)
    normed_one, unit_one, inverse_one = norm_forward(inputs, norm_gain[0], norm_shift[0])
    starts = run_starts(segment_ids)
    cosine, sine = rotary_tables(starts)
    wheres = [where_of([(z - p) % n for z in range(n)]) for p in range(n)]

    wheres_back = [where_of(list(range(n)))] + [
        where_of([z + d if above else z - d for z, (d, above) in enumerate(column)])
        for column in zip(*arrivals)
    ]

    rows_one = [normed_one.astype(BF16)]
    buffer = None
    for p in range(n):
        if p < n - 1:
            moved = pass_on(rows_one[p])
            rows_one.append(
                after(moved, cosine, sine, starts, *wheres, *wheres_back) if p == 0 else moved
            )
        pre = contract(rows_one[p], w_qkv, 1, 1) + qkv_bias.reshape(1, 3 * width)
        buffer = rope_block(wheres[p], pre, cosine, sine, buffer, width, length)

    cotangent = after(output_grad, rows_one[n - 1])
    grad_up, grad_down_way = [cotangent], [cotangent]
    for hop in range(1, n):
        grad_up.append(pass_up(grad_up[hop - 1], hop - 1, n - 2))
        grad_down_way.append(pass_down(grad_down_way[hop - 1], 1, n - hop))

    mixed, totals, parts, lows = [None] * n, [None] * n, [None] * n, [None] * n
    gate = None
    for p in [1, *range(n - 1, 1, -1), 0]:
        where = wheres[p] if gate is None else after(wheres[p], gate)
        mixed[p], totals[p] = attend_block(where, starts, buffer, block)
        term = contract(mixed[p], w_proj, 0, 0)
        parts[p], lows[p] = apart(term, term.astype(BF16)) if p in (1, n - 1) else (term, None)
        gate = parts[p]

    def scatter_chains(parts, lows, gate=()):
        up = down = None
        for step in range(n - 1):
            term_up, term_down = parts[step + 1], parts[n - 1 - step]
            send_up = lows[1] if up is None else plus(term_up, up)
            send_down = lows[n - 1] if down is None else plus(term_down, after(down, send_up))
            if step == 0 and gate:
                send_up, send_down = after(send_up, *gate), after(send_down, *gate)
            up = pass_up(send_up, 0, step)
            down = pass_down(send_down, n - 1 - step, n - 1)
        return parts[0] + up.astype(F32) + down.astype(F32)

    middle = inputs + scatter_chains(parts, lows)
    grad_rows = [output_grad] + [
        jnp.where(place >= p, grad_up[p], grad_down_way[n - p]) for p in range(1, n)
    ]

    normed_two, unit_two, inverse_two = norm_forward(middle, norm_gain[1], norm_shift[1])
    rows_two = [normed_two.astype(BF16)]
    hidden, gate_grads, upper_grads, out_parts, back_parts = [], [], [], [], []
    out_lows, back_lows = [], []
    for p in range(n):
        if p < n - 1:
            rows_two.append(pass_on(rows_two[p]))
        gate = jnp.dot(rows_two[p], w_feed[0], preferred_element_type=F32)
        upper = jnp.dot(rows_two[p], w_feed[1], preferred_element_type=F32)
        grad_hidden = contract(grad_rows[p], w_down, 1, 1)
        sigma = jax.nn.sigmoid(gate)
        swish = gate * sigma
        hidden_low = (swish * upper).astype(BF16)
        gate_low = (grad_hidden * upper * sigma * (1.0 + gate * (1.0 - sigma))).astype(BF16)
        upper_low = (grad_hidden * swish).astype(BF16)
        hidden_low, gate_low, upper_low = apart(hidden_low, gate_low, upper_low)
        hidden.append(hidden_low)
        gate_grads.append(gate_low)
        upper_grads.append(upper_low)
        term = contract(gate_low, w_feed[0], 1, 1) + contract(upper_low, w_feed[1], 1, 1)
        if p == 1:
            term, low = apart(term, term.astype(BF16))
        else:
            (term,), low = apart(term), None
        back_parts.append(term)
        back_lows.append(low)
        term = jnp.dot(hidden_low, w_down, preferred_element_type=F32)
        if p in (1, n - 1):
            term, low = apart(term, term.astype(BF16))
        else:
            (term,), low = apart(term), None
        out_parts.append(term)
        out_lows.append(low)

    def scatter_sum(grad, axis):
        return lax.psum_scatter(grad, "dp", scatter_dimension=axis, tiled=True).astype(F32)

    grad_down = contract(
        jnp.concatenate(hidden, axis=0), jnp.concatenate(grad_rows, axis=0), 0, 0
    ).astype(BF16)
    down_sum = scatter_sum(grad_down, 1)
    grad_feed = jnp.einsum(
        "rd,krf->kdf",
        jnp.concatenate(rows_two, axis=0),
        jnp.concatenate(gate_grads + upper_grads, axis=0).reshape(2, length, units),
        preferred_element_type=F32,
    ).astype(BF16)
    feed_sum = scatter_sum(grad_feed, 1)

    moving = None
    for step in range(1, n):
        send = back_lows[step] if moving is None else plus(back_parts[step], moving)
        moving = pass_on(send)
    grad_normed_two = back_parts[0] + moving.astype(F32)

    grad_middle = output_grad.astype(F32) + norm_backward(
        grad_normed_two, unit_two, inverse_two, norm_gain[1]
    )
    gain_two = jnp.sum(grad_normed_two * unit_two, axis=0)
    shift_two = jnp.sum(grad_normed_two, axis=0)

    own = grad_middle.astype(BF16)
    ups, downs = [own], [own]
    all_totals = jnp.concatenate(totals, axis=0)
    slots, before = [own], None

    def back_block(slot, last):
        grad_mixed = contract(w_proj, slots[slot], 1, 1).astype(BF16)
        return attend_back_block(
            wheres_back[slot],
            starts,
            cosine,
            sine,
            buffer,
            grad_mixed,
            all_totals,
            before,
            last,
        )

    for hop in range(1, n):
        ups.append(pass_up(ups[hop - 1], hop - 1, n - 2))
        downs.append(pass_down(downs[hop - 1], 1, n - hop))
        before = back_block(hop - 1, False)
        chosen, here = None, after(place, slots[hop - 1])
        for z in range(n):
            d, above = arrivals[z][hop - 1]
            value = downs[d] if above else ups[d]
            chosen = value if chosen is None else jnp.where(here == z, value, chosen)
        slots.append(apart(chosen)[0])
    grad_pre = back_block(n - 1, True)
    layer_output = middle + scatter_chains(out_parts, out_lows, (ups[1], downs[1]))

    flat_pre = grad_pre.reshape(3 * width, length)
    moving = None
    for step in [*range(1, n), 0]:
        term = contract(flat_pre[:, step * block : (step + 1) * block], w_qkv, 0, 0)
        if step == 0:
            grad_normed_one = term + moving.astype(F32)
        else:
            send = term.astype(BF16) if moving is None else plus(term, moving)
            moving = pass_on(send)
    grad_qkv = contract(flat_pre, jnp.concatenate(rows_one, axis=0), 1, 0).astype(BF16)
    all_mixed = jnp.concatenate(mixed, axis=1)
    mixed_slots = []
    for slot in range(n):
        at = [0] * n if slot == 0 else [
            (-d if above else d) % n for d, above in (arrivals[z][slot - 1] for z in range(n))
        ]
        mixed_slots.append(
            lax.dynamic_slice_in_dim(all_mixed, at_place(at) * block, block, 1)
        )
    grad_proj = contract(
        jnp.concatenate(mixed_slots, axis=1), jnp.concatenate(slots, axis=0), 1, 0
    ).astype(BF16)
    grad_both = jnp.concatenate([grad_qkv, grad_proj], axis=0)
    both_rows = scatter_sum(grad_both, 1)
    qkv_sum = both_rows[: 3 * width].reshape(3, width, depth // data_size).transpose(0, 2, 1)
    proj_sum = both_rows[3 * width :]

    bias_local = jnp.sum(grad_pre.astype(F32), axis=2)
    input_grad = grad_middle + norm_backward(grad_normed_one, unit_one, inverse_one, norm_gain[0])
    gain_one = jnp.sum(grad_normed_one * unit_one, axis=0)
    shift_one = jnp.sum(grad_normed_one, axis=0)

    def sum_over(values, axis, size):
        step = 1
        while step < size:
            values = values + lax.ppermute(values, axis, [(i, i ^ step) for i in range(size)])
            step *= 2
        return values

    small = jnp.concatenate(
        [gain_one, gain_two, shift_one, shift_two, bias_local.reshape(3 * width)]
    )
    small = sum_over(small.reshape(-1, 128), "dp", data_size).reshape(-1)
    bias_grad = small[4 * depth :].reshape(3, width)
    small = sum_over(small[: 4 * depth].reshape(-1, 128), "tensor", n)
    gain_total, shift_total = small.reshape(2, 2, depth)

    outputs = [layer_output, input_grad]
    groups = (
        (norm_gain, gain_total, gain_mean, gain_square),
        (norm_shift, shift_total, shift_mean, shift_square),
        (qkv_bias, bias_grad, bias_mean, bias_square),
        (qkv_weight, qkv_sum, qkv_mean, qkv_square),
        (proj_weight, proj_sum, proj_mean, proj_square),
        (feed_weight, feed_sum, feed_mean, feed_square),
        (down_weight, down_sum, down_mean, down_square),
    )
    for which, (param_arr, grad_total, mean_in, square_in) in enumerate(groups):
        change, mean_new, square_new = adamw(param_arr, grad_total, mean_in, square_in)
        shown = change if which < 3 else param_arr + change
        outputs.extend([grad_total, shown, mean_new, square_new])
    return tuple(outputs)


def solution(mesh):
    tokens, small, bias = P(("dp", "tensor"), None), P(), P(None, "tensor")
    three, two = P(None, "dp", "tensor"), P("tensor", "dp")
    per_param = [small] * 6 + [bias] * 3 + [three] * 3 + [two] * 3 + [three] * 3 + [two] * 3
    outs = [small] * 8 + [bias] * 4 + [three] * 4 + [two] * 4 + [three] * 4 + [two] * 4
    n = mesh.shape["tensor"]

    def body(*args):
        return per_device(n, mesh.shape["dp"], *args)

    return jax.shard_map(
        body,
        mesh=mesh,
        in_specs=(tokens, tokens, P("dp", None), *per_param),
        out_specs=(tokens, tokens, *outs),
        check_vma=False,
    )
```

profile of v0, /device:TPU:0, one launch (start us, length us, event | category | flops | bytes accessed | tf_op | source)
XLA Modules:
  0.0 827.6 jit_solution(8840330670703275138)
XLA Ops:
  35.9 8.9 %collective-permute-done = bf16[256,2048]{1,0:T(8,128)(2,1)S(1)} collective-permute-done((bf16[256,2048]{1,0:T(8,128)(2,1)S(1)}, bf16[256,2048]{1,0:T(8,128)(2,1)S(1)}, u32[]{:S(2)}, u32[]{:S(2)}) %collective-permute-start) | collective-permute-done | bytes 1048608 | tf_op jit(solution)/shard_map/ppermute | solution.py:383
  44.8 26.2 %collective-permute-done.1 = bf16[256,2048]{1,0:T(8,128)(2,1)} collective-permute-done((bf16[256,2048]{1,0:T(8,128)(2,1)S(1)}, bf16[256,2048]{1,0:T(8,128)(2,1)}, u32[]{:S(2)}, u32[]{:S(2)}) %collective-permute-start.1) | collective-permute-done | bytes 1048608 | tf_op jit(solution)/shard_map/ppermute | solution.py:383
  108.3 7.9 attend_block.4
  159.4 14.0 %collective-permute-done.4 = bf16[256,2048]{1,0:T(8,128)(2,1)S(1)} collective-permute-done((bf16[256,2048]{1,0:T(8,128)(2,1)S(1)}, bf16[256,2048]{1,0:T(8,128)(2,1)S(1)}, u32[]{:S(2)}, u32[]{:S(2)}) %collective-permute-start.4) | collective-permute-done | bytes 1048608 | tf_op jit(solution)/shard_map/ppermute | solution.py:383
  177.2 15.0 %collective-permute-start.5 = (bf16[256,2048]{1,0:T(8,128)(2,1)}, bf16[256,2048]{1,0:T(8,128)(2,1)}, u32[]{:S(2)}, u32[]{:S(2)}) collective-permute-start(bf16[256,2048]{1,0:T(8,128)(2,1)} %add_convert_fusion.11), channel_id=1, source_target_pairs={{0,1},{1,2},{2,3},{4,5},{5,6},{6,7},{8,9},{9,10},{10,11},{12,13},{... | collective-permute-start | bytes 3145736 | tf_op jit(solution)/shard_map/ppermute | solution.py:383
  218.9 38.6 %collective-permute-start.9 = (bf16[256,2048]{1,0:T(8,128)(2,1)}, bf16[256,2048]{1,0:T(8,128)(2,1)}, u32[]{:S(2)}, u32[]{:S(2)}) collective-permute-start(bf16[256,2048]{1,0:T(8,128)(2,1)} %add_convert_fusion.8), channel_id=1, source_target_pairs={{0,1},{1,2},{2,3},{3,0},{4,5},{5,6},{6,7},{7,4},{8,9},{9,10},{10,1... | collective-permute-start | bytes 3145736 | tf_op jit(solution)/shard_map/ppermute | solution.py:383
  259.6 10.6 %collective-permute-done.9 = bf16[256,2048]{1,0:T(8,128)(2,1)} collective-permute-done((bf16[256,2048]{1,0:T(8,128)(2,1)}, bf16[256,2048]{1,0:T(8,128)(2,1)}, u32[]{:S(2)}, u32[]{:S(2)}) %collective-permute-start.9) | collective-permute-done | bytes 1048608 | tf_op jit(solution)/shard_map/ppermute | solution.py:383
  270.2 27.5 %collective-permute-start.10 = (bf16[256,2048]{1,0:T(8,128)(2,1)}, bf16[256,2048]{1,0:T(8,128)(2,1)}, u32[]{:S(2)}, u32[]{:S(2)}) collective-permute-start(bf16[256,2048]{1,0:T(8,128)(2,1)} %collective-permute-done.9), channel_id=1, source_target_pairs={{0,1},{1,2},{2,3},{3,0},{4,5},{5,6},{6,7},{7,4},{8,9},{9,10},{10,1... | collective-permute-start | bytes 3145736 | tf_op jit(solution)/shard_map/ppermute | solution.py:383
  300.0 17.4 %collective-permute-done.17 = bf16[256,2048]{1,0:T(8,128)(2,1)S(1)} collective-permute-done((bf16[256,2048]{1,0:T(8,128)(2,1)}, bf16[256,2048]{1,0:T(8,128)(2,1)S(1)}, u32[]{:S(2)}, u32[]{:S(2)}) %collective-permute-start.17) | collective-permute-done | bytes 1048608 | tf_op jit(solution)/shard_map/ppermute | solution.py:383
  328.9 32.8 %collective-permute-done.11 = bf16[256,2048]{1,0:T(8,128)(2,1)} collective-permute-done((bf16[256,2048]{1,0:T(8,128)(2,1)}, bf16[256,2048]{1,0:T(8,128)(2,1)}, u32[]{:S(2)}, u32[]{:S(2)}) %collective-permute-start.11) | collective-permute-done | bytes 1048608 | tf_op jit(solution)/shard_map/ppermute | solution.py:383
  404.1 9.0 %convolution_convert_fusion = bf16[1408,2048]{1,0:T(8,128)(2,1)} fusion(bf16[256,2048]{1,0:T(8,128)(2,1)S(1)} %copy-done.26, bf16[256,2048]{1,0:T(8,128)(2,1)S(1)} %copy-done.24, bf16[256,2048]{1,0:T(8,128)(2,1)S(1)} %copy-done.25, bf16[256,2048]{1,0:T(8,128)(2,1)S(1)} %copy-done.18, bf16[256,1408]{1,0:T(8,128)(2,1)S(1)} %get-tuple-element.95, ...), kind=kOutput, calls=%fused_computation.2 | convolution fusion | flops 5936775168 | bytes 12845056 | tf_op jit(solution)/shard_map/dot_general | solution.py:66
  426.3 17.2 %convert_bitcast_fusion = bf16[2,2048,1408]{1,2,0:T(8,128)(2,1)} fusion(bf16[2,1024,1408]{2,1,0:T(8,128)(2,1)S(1)} %bitcast.173, bf16[256,2048]{1,0:T(8,128)(2,1)} %collective-permute-done.11, bf16[256,2048]{1,0:T(8,128)(2,1)} %collective-permute-done.10, bf16[256,2048]{1,0:T(8,128)(2,1)} %collective-permute-done.9, bf16[256,2048]{1,0:T(8,128)(2,1)} %add_convert_fusion.8), kind=kOutput, calls=%fused_computation | convolution fusion | flops 11833704448 | bytes 21495808 | tf_op jit(solution)/shard_map/rd,krf->kdf/dot_general | solution.py:513
  463.3 19.6 %collective-permute-done.18 = bf16[256,2048]{1,0:T(8,128)(2,1)S(1)} collective-permute-done((bf16[256,2048]{1,0:T(8,128)(2,1)S(1)}, bf16[256,2048]{1,0:T(8,128)(2,1)S(1)}, u32[]{:S(2)}, u32[]{:S(2)}) %collective-permute-start.18) | collective-permute-done | bytes 1048608 | tf_op jit(solution)/shard_map/ppermute | solution.py:383
  487.0 19.0 %collective-permute-done.19 = bf16[256,2048]{1,0:T(8,128)(2,1)S(1)} collective-permute-done((bf16[256,2048]{1,0:T(8,128)(2,1)S(1)}, bf16[256,2048]{1,0:T(8,128)(2,1)S(1)}, u32[]{:S(2)}, u32[]{:S(2)}) %collective-permute-start.19) | collective-permute-done | bytes 1048608 | tf_op jit(solution)/shard_map/ppermute | solution.py:383
  513.3 14.9 %collective-permute-done.20 = bf16[256,2048]{1,0:T(8,128)(2,1)S(1)} collective-permute-done((bf16[256,2048]{1,0:T(8,128)(2,1)S(1)}, bf16[256,2048]{1,0:T(8,128)(2,1)S(1)}, u32[]{:S(2)}, u32[]{:S(2)}) %collective-permute-start.20) | collective-permute-done | bytes 1048608 | tf_op jit(solution)/shard_map/ppermute | solution.py:383
  562.7 7.7 collective-permute-start.23
  573.1 9.2 %attend_back_block.5 = (bf16[512,1024]{1,0:T(8,128)(2,1)}, f32[2,512,1024]{2,1,0:T(8,128)}) custom-call(s32[3]{0:T(128)} %get-tuple-element.261.where_ref, s32[1,1024]{1,0:T(1,128)} %reduce_window_max.25.starts_ref, f32[8,1024]{1,0:T(8,128)} %get-tuple-element.245.c.cos_ref.refs_0_, ...), custom_call_target="tpu_custom_call", output_to_operand_aliasing={{0}: (9, {}), {1}: (10, {})} | custom-call | flops 5368709120 | bytes 11272192 | tf_op jit(solution)/shard_map/attend_back_block/pallas_call | solution.py:327
  590.3 10.3 %attend_back_block.6 = (bf16[512,1024]{1,0:T(8,128)(2,1)}, f32[2,512,1024]{2,1,0:T(8,128)}) custom-call(s32[3]{0:T(128)} %get-tuple-element.262.where_ref, s32[1,1024]{1,0:T(1,128)} %reduce_window_max.25.starts_ref, f32[8,1024]{1,0:T(8,128)} %get-tuple-element.245.c.cos_ref.refs_0_, ...), custom_call_target="tpu_custom_call", output_to_operand_aliasing={{0}: (9, {}), {1}: (10, {})} | custom-call | flops 5368709120 | bytes 11272192 | tf_op jit(solution)/shard_map/attend_back_block/pallas_call | solution.py:327
  603.5 11.9 %attend_back_block.7 = bf16[3,512,1024]{2,1,0:T(8,128)(2,1)} custom-call(s32[3]{0:T(128)} %add_add_fusion.7.where_ref, s32[1,1024]{1,0:T(1,128)} %reduce_window_max.25.starts_ref, f32[8,1024]{1,0:T(8,128)} %get-tuple-element.245.c.cos_ref.refs_0_, f32[8,1024]{1,0:T(8,128)} %get-tuple-element.244.d.sin_ref.refs_1_, ...), custom_call_target="tpu_custom_call" | custom-call | flops 5368709120 | bytes 11272192 | tf_op jit(solution)/shard_map/attend_back_block/pallas_call | solution.py:327
  615.6 11.1 %convolution_convert_fusion.1 = bf16[1536,2048]{1,0:T(8,128)(2,1)} fusion(bf16[1536,1024]{1,0:T(8,128)(2,1)} %bitcast.161, bf16[256,2048]{1,0:T(8,128)(2,1)} %collective-permute-done.2, bf16[256,2048]{1,0:T(8,128)(2,1)} %collective-permute-done.1, bf16[256,2048]{1,0:T(8,128)(2,1)S(1)} %copy-done.78, bf16[256,2048]{1,0:T(8,128)(2,1)S(1)} %copy-done.21), kind=kOutput, calls=%fused_computation.3 | convolution fusion | flops 6462373888 | bytes 13631488 | tf_op jit(solution)/shard_map/dot_general | solution.py:66
  678.4 13.6 %collective-permute-done.33 = bf16[256,2048]{1,0:T(8,128)(2,1)} collective-permute-done((bf16[256,2048]{1,0:T(8,128)(2,1)}, bf16[256,2048]{1,0:T(8,128)(2,1)}, u32[]{:S(2)}, u32[]{:S(2)}) %collective-permute-start.33) | collective-permute-done | bytes 1048608 | tf_op jit(solution)/shard_map/ppermute | solution.py:383
  697.6 8.2 collective-permute-start.34
  711.8 20.8 %collective-permute-done.34 = bf16[256,2048]{1,0:T(8,128)(2,1)S(1)} collective-permute-done((bf16[256,2048]{1,0:T(8,128)(2,1)S(1)}, bf16[256,2048]{1,0:T(8,128)(2,1)S(1)}, u32[]{:S(2)}, u32[]{:S(2)}) %collective-permute-start.34) | collective-permute-done | bytes 1048608 | tf_op jit(solution)/shard_map/ppermute | solution.py:383
  789.7 8.7 %multiply_add_fusion = (f32[2,256,1408]{1,2,0:T(8,128)}, f32[2,256,1408]{1,2,0:T(8,128)}, f32[2,256,1408]{1,2,0:T(8,128)S(1)}) fusion(f32[2,256,1408]{1,2,0:T(8,128)} %copy.97, bf16[2,256,1408]{1,2,0:T(8,128)(2,1)} %reduce-scatter.6.cloned.1.call-done, f32[2,256,1408]{1,2,0:T(8,128)} %copy.94, f32[2,256,1408]{1,2,0:T(8,128)} %copy.95), kind=kLoop, calls=%fused_computation.49 | loop fusion | flops 11534336 | bytes 18743296 | tf_op jit(solution)/shard_map/add | solution.py:624
  (486 shorter events, 425.4 us)
Async XLA Ops:
  7.2 64.3 %all-gather.5.cloned.1.call-start = ((), (), s32[]{:S(2)}) async-start(), calls=%async_computation.3 | async-start | bytes 7077888 | tf_op jit(solution)/shard_map/all_gather | solution.py:409
  10.0 106.2 %all-gather.7.cloned.1.call-start = ((), (), s32[]{:S(2)}) async-start(), calls=%async_computation.4 | async-start | bytes 2359296 | tf_op jit(solution)/shard_map/all_gather | solution.py:409
  10.8 312.5 %all-gather.11.cloned.1.call-start = ((), (), s32[]{:S(2)}) async-start(), calls=%async_computation.6 | async-start | bytes 6488064 | tf_op jit(solution)/shard_map/all_gather | solution.py:409
  11.8 349.9 %all-gather.9.cloned.1.call-start = ((), (), s32[]{:S(2)}) async-start(), calls=%async_computation.5 | async-start | bytes 12976128 | tf_op jit(solution)/shard_map/all_gather | solution.py:409
  15.1 744.6 %reduce-scatter.8.cloned.1.call-start = ((), (), s32[]{:S(2)}) async-start(), calls=%async_computation.9 | async-start | bytes 6488064 | tf_op jit(solution)/shard_map/reduce_scatter | solution.py:507
  152.5 39.7 %collective-permute-start.15 = (bf16[256,2048]{1,0:T(8,128)(2,1)S(1)}, bf16[256,2048]{1,0:T(8,128)(2,1)}, u32[]{:S(2)}, u32[]{:S(2)}) collective-permute-start(bf16[256,2048]{1,0:T(8,128)(2,1)S(1)} %copy-done.17), channel_id=1, source_target_pairs={{1,0},{2,1},{3,2},{5,4},{6,5},{7,6},{9,8},{10,9},{11,10},{13,12},{... | collective-permute-start | bytes 3145736 | tf_op jit(solution)/shard_map/ppermute | solution.py:383
  153.8 42.0 %collective-permute-start.12 = (bf16[256,2048]{1,0:T(8,128)(2,1)S(1)}, bf16[256,2048]{1,0:T(8,128)(2,1)}, u32[]{:S(2)}, u32[]{:S(2)}) collective-permute-start(bf16[256,2048]{1,0:T(8,128)(2,1)S(1)} %copy-done.17), channel_id=1, source_target_pairs={{0,1},{1,2},{2,3},{4,5},{5,6},{6,7},{8,9},{9,10},{10,11},{12,13},{... | collective-permute-start | bytes 3145736 | tf_op jit(solution)/shard_map/ppermute | solution.py:383
  175.9 32.4 %collective-permute-start.8 = (bf16[256,2048]{1,0:T(8,128)(2,1)}, bf16[256,2048]{1,0:T(8,128)(2,1)}, u32[]{:S(2)}, u32[]{:S(2)}) collective-permute-start(bf16[256,2048]{1,0:T(8,128)(2,1)} %add_convert_fusion.9), channel_id=1, source_target_pairs={{1,0},{2,1},{3,2},{5,4},{6,5},{7,6},{9,8},{10,9},{11,10},{13,12},{... | collective-permute-start | bytes 3145736 | tf_op jit(solution)/shard_map/ppermute | solution.py:383
  177.2 37.8 %collective-permute-start.5 = (bf16[256,2048]{1,0:T(8,128)(2,1)}, bf16[256,2048]{1,0:T(8,128)(2,1)}, u32[]{:S(2)}, u32[]{:S(2)}) collective-permute-start(bf16[256,2048]{1,0:T(8,128)(2,1)} %add_convert_fusion.11), channel_id=1, source_target_pairs={{0,1},{1,2},{2,3},{4,5},{5,6},{6,7},{8,9},{9,10},{10,11},{12,13},{... | collective-permute-start | bytes 3145736 | tf_op jit(solution)/shard_map/ppermute | solution.py:383
  192.2 65.4 %collective-permute-start.16 = (bf16[256,2048]{1,0:T(8,128)(2,1)}, bf16[256,2048]{1,0:T(8,128)(2,1)}, u32[]{:S(2)}, u32[]{:S(2)}) collective-permute-start(bf16[256,2048]{1,0:T(8,128)(2,1)} %collective-permute-done.15), channel_id=1, source_target_pairs={{1,0},{2,1},{5,4},{6,5},{9,8},{10,9},{13,12},{14,13},{17,16},{18,1... | collective-permute-start | bytes 3145736 | tf_op jit(solution)/shard_map/ppermute | solution.py:383
  195.8 63.0 %collective-permute-start.13 = (bf16[256,2048]{1,0:T(8,128)(2,1)}, bf16[256,2048]{1,0:T(8,128)(2,1)}, u32[]{:S(2)}, u32[]{:S(2)}) collective-permute-start(bf16[256,2048]{1,0:T(8,128)(2,1)} %collective-permute-done.12), channel_id=1, source_target_pairs={{1,2},{2,3},{5,6},{6,7},{9,10},{10,11},{13,14},{14,15},{17,18},{18... | collective-permute-start | bytes 3145736 | tf_op jit(solution)/shard_map/ppermute | solution.py:383
  218.9 51.2 %collective-permute-start.9 = (bf16[256,2048]{1,0:T(8,128)(2,1)}, bf16[256,2048]{1,0:T(8,128)(2,1)}, u32[]{:S(2)}, u32[]{:S(2)}) collective-permute-start(bf16[256,2048]{1,0:T(8,128)(2,1)} %add_convert_fusion.8), channel_id=1, source_target_pairs={{0,1},{1,2},{2,3},{3,0},{4,5},{5,6},{6,7},{7,4},{8,9},{9,10},{10,1... | collective-permute-start | bytes 3145736 | tf_op jit(solution)/shard_map/ppermute | solution.py:383
  257.5 59.9 %collective-permute-start.17 = (bf16[256,2048]{1,0:T(8,128)(2,1)}, bf16[256,2048]{1,0:T(8,128)(2,1)S(1)}, u32[]{:S(2)}, u32[]{:S(2)}) collective-permute-start(bf16[256,2048]{1,0:T(8,128)(2,1)} %collective-permute-done.16), channel_id=1, source_target_pairs={{1,0},{5,4},{9,8},{13,12},{17,16},{21,20},{25,24},{29,28}} | collective-permute-start | bytes 3145736 | tf_op jit(solution)/shard_map/ppermute | solution.py:383
  258.8 62.2 %collective-permute-start.14 = (bf16[256,2048]{1,0:T(8,128)(2,1)}, bf16[256,2048]{1,0:T(8,128)(2,1)S(1)}, u32[]{:S(2)}, u32[]{:S(2)}) collective-permute-start(bf16[256,2048]{1,0:T(8,128)(2,1)} %collective-permute-done.13), channel_id=1, source_target_pairs={{2,3},{6,7},{10,11},{14,15},{18,19},{22,23},{26,27},{30,31}} | collective-permute-start | bytes 3145736 | tf_op jit(solution)/shard_map/ppermute | solution.py:383
  270.2 48.3 %collective-permute-start.10 = (bf16[256,2048]{1,0:T(8,128)(2,1)}, bf16[256,2048]{1,0:T(8,128)(2,1)}, u32[]{:S(2)}, u32[]{:S(2)}) collective-permute-start(bf16[256,2048]{1,0:T(8,128)(2,1)} %collective-permute-done.9), channel_id=1, source_target_pairs={{0,1},{1,2},{2,3},{3,0},{4,5},{5,6},{6,7},{7,4},{8,9},{9,10},{10,1... | collective-permute-start | bytes 3145736 | tf_op jit(solution)/shard_map/ppermute | solution.py:383
  318.5 43.2 %collective-permute-start.11 = (bf16[256,2048]{1,0:T(8,128)(2,1)}, bf16[256,2048]{1,0:T(8,128)(2,1)}, u32[]{:S(2)}, u32[]{:S(2)}) collective-permute-start(bf16[256,2048]{1,0:T(8,128)(2,1)} %collective-permute-done.10), channel_id=1, source_target_pairs={{0,1},{1,2},{2,3},{3,0},{4,5},{5,6},{6,7},{7,4},{8,9},{9,10},{10,1... | collective-permute-start | bytes 3145736 | tf_op jit(solution)/shard_map/ppermute | solution.py:383
  413.1 376.6 %reduce-scatter.6.cloned.1.call-start = ((), (), s32[]{:S(2)}) async-start(), calls=%async_computation.8 | async-start | bytes 12976128 | tf_op jit(solution)/shard_map/reduce_scatter | solution.py:507
  443.5 367.1 %reduce-scatter.4.cloned.1.call-start = ((), (), s32[]{:S(2)}) async-start(), calls=%async_computation.7 | async-start | bytes 9437184 | tf_op jit(solution)/shard_map/reduce_scatter | solution.py:507
  561.1 85.6 %collective-permute-start.26 = (bf16[256,2048]{1,0:T(8,128)(2,1)}, bf16[256,2048]{1,0:T(8,128)(2,1)}, u32[]{:S(2)}, u32[]{:S(2)}) collective-permute-start(bf16[256,2048]{1,0:T(8,128)(2,1)} %get-tuple-element.112), channel_id=1, source_target_pairs={{3,2},{7,6},{11,10},{15,14},{19,18},{23,22},{27,26},{31,30}} | collective-permute-start | bytes 3145736 | tf_op jit(solution)/shard_map/ppermute | solution.py:383
  562.7 75.3 %collective-permute-start.23 = (bf16[256,2048]{1,0:T(8,128)(2,1)}, bf16[256,2048]{1,0:T(8,128)(2,1)}, u32[]{:S(2)}, u32[]{:S(2)}) collective-permute-start(bf16[256,2048]{1,0:T(8,128)(2,1)} %get-tuple-element.109), channel_id=1, source_target_pairs={{0,1},{4,5},{8,9},{12,13},{16,17},{20,21},{24,25},{28,29}} | collective-permute-start | bytes 3145736 | tf_op jit(solution)/shard_map/ppermute | solution.py:383
  656.0 36.1 %collective-permute-start.33 = (bf16[256,2048]{1,0:T(8,128)(2,1)}, bf16[256,2048]{1,0:T(8,128)(2,1)}, u32[]{:S(2)}, u32[]{:S(2)}) collective-permute-start(bf16[256,2048]{1,0:T(8,128)(2,1)} %convolution_convert_fusion.2), channel_id=1, source_target_pairs={{0,1},{1,2},{2,3},{3,0},{4,5},{5,6},{6,7},{7,4},{8,9},{9,10},{10,1... | collective-permute-start | bytes 3145736 | tf_op jit(solution)/shard_map/ppermute | solution.py:383
  672.8 70.1 %collective-permute-start.25 = (bf16[256,2048]{1,0:T(8,128)(2,1)}, bf16[256,2048]{1,0:T(8,128)(2,1)}, u32[]{:S(2)}, u32[]{:S(2)}) collective-permute-start(bf16[256,2048]{1,0:T(8,128)(2,1)} %add_convert_fusion.4), channel_id=1, source_target_pairs={{0,1},{1,2},{2,3},{4,5},{5,6},{6,7},{8,9},{9,10},{10,11},{12,13},{... | collective-permute-start | bytes 3145736 | tf_op jit(solution)/shard_map/ppermute | solution.py:383
  697.6 34.9 %collective-permute-start.34 = (bf16[256,2048]{1,0:T(8,128)(2,1)S(1)}, bf16[256,2048]{1,0:T(8,128)(2,1)S(1)}, u32[]{:S(2)}, u32[]{:S(2)}) collective-permute-start(bf16[256,2048]{1,0:T(8,128)(2,1)S(1)} %add_convert_fusion.1), channel_id=1, source_target_pairs={{0,1},{1,2},{2,3},{3,0},{4,5},{5,6},{6,7},{7,4},{8,9},{9,10},{10,1... | collective-permute-start | bytes 3145736 | tf_op jit(solution)/shard_map/ppermute | solution.py:383
  708.3 34.6 %collective-permute-start.28 = (bf16[256,2048]{1,0:T(8,128)(2,1)}, bf16[256,2048]{1,0:T(8,128)(2,1)}, u32[]{:S(2)}, u32[]{:S(2)}) collective-permute-start(bf16[256,2048]{1,0:T(8,128)(2,1)} %add_convert_fusion.2), channel_id=1, source_target_pairs={{1,0},{2,1},{3,2},{5,4},{6,5},{7,6},{9,8},{10,9},{11,10},{13,12},{... | collective-permute-start | bytes 3145736 | tf_op jit(solution)/shard_map/ppermute | solution.py:383
  (137 other events, 2165.1 us)
Sparse Core Ops, SparseCore 0:
  10.5 49.3 all-gather.4
  62.3 28.0 all-gather.6
  92.9 44.2 all-gather.10
  139.5 67.5 all-gather.8
  413.2 56.5 reduce-scatter.7
  473.2 86.8 reduce-scatter.5
  638.1 69.4 reduce-scatter.3
where the time goes:
time: 833 us; the launch traced here: 828 us
  waiting for transfers between devices  242 us (29%)
  matrix products  183 us (22%)
  starting transfers between devices  165 us (20%)
  other arithmetic  92.5 us (11%)
  Pallas kernels  77.7 us (9%)
  local copies, waits for them, and re-layouts  45.6 us (5%)
  between operations  22.2 us (3%)
    ppermute x36, waiting for transfers between devices, pass_on(): return lax.ppermute(values, 'tensor', pairs)  229 us
    ppermute x36, starting transfers between devices, pass_on(): return lax.ppermute(values, 'tensor', pairs)  157 us
    dot_general x31, matrix products, contract(): lax.dot_general(left, right, (((left_dim,), (right_dim,)), ((), ())), pre...  122 us
    pallas_call x4, Pallas kernels, attend_back_block(): pl.pallas_call(functools.partial(attend_back_kernel, blocks, block, first...  38.6 us
    unnamed x251, local copies, waits for them, and re-layouts  33.2 us
    pallas_call x4, Pallas kernels, attend_block(): pl.pallas_call(functools.partial(attend_kernel, blocks, block), out_shape...  26.6 us
    add x4, other arithmetic, per_device(): shown = change if which < 3 else param_arr + change  21.1 us
    convert_element_type x10, other arithmetic, plus(): return (term + moving.astype(F32)).astype(BF16)  18.9 us
  transfers between devices with their start and end apart: 48, of which 22 were waited for; matrix products, arithmetic and copies ran while one was open for 31% of the time, Pallas kernels for 9%

commit v1 on v0

--- a/solution.py
+++ b/solution.py
@@ -5,6 +5,7 @@
 import jax.numpy as jnp
 from jax import lax
 from jax.experimental import pallas as pl
+from jax.experimental.layout import Layout, with_layout_constraint
 from jax.experimental.pallas import tpu as pltpu
 from jax.sharding import PartitionSpec as P
 
@@ -91,7 +92,7 @@
             out_ref[which, rows, :] = part.astype(BF16)
 
 
-def rope_block(where, pre, cosine, sine, buffer, width, length):
+def rope_block(where, base, pre, cosine, sine, buffer, width, length):
     rows = WIDE * HEAD
     groups = width // rows
     block = pre.shape[0]
@@ -101,8 +102,8 @@
         pl.BlockSpec((block, rows), lambda h, s: (0, h)),
         pl.BlockSpec((block, rows), lambda h, s: (0, groups + h)),
         pl.BlockSpec((block, rows), lambda h, s: (0, 2 * groups + h)),
-        pl.BlockSpec((HALF, block), lambda h, s: (0, s[0])),
-        pl.BlockSpec((HALF, block), lambda h, s: (0, s[0])),
+        pl.BlockSpec((HALF, block), lambda h, s: (0, s[base])),
+        pl.BlockSpec((HALF, block), lambda h, s: (0, s[base])),
     ]
     args = [where, pre, pre, pre, cosine, sine]
     aliases = {}
@@ -119,7 +120,7 @@
             num_scalar_prefetch=1,
             grid=(groups,),
             in_specs=specs,
-            out_specs=pl.BlockSpec((3, rows, block), lambda h, s: (0, h, s[0])),
+            out_specs=pl.BlockSpec((3, rows, block), lambda h, s: (0, h, s[base])),
         ),
         input_output_aliases=aliases,
         cost_estimate=pl.CostEstimate(
@@ -139,11 +140,11 @@
     return mask
 
 
-def attend_kernel(blocks, block, where_ref, starts_ref, q_ref, k_ref, v_ref, out_ref, total_ref):
+def attend_kernel(blocks, block, base, where_ref, starts_ref, q_ref, k_ref, v_ref, out_ref, total_ref):
     starts = starts_ref[...]
     for mine in range(blocks):
 
-        @pl.when(where_ref[0] == mine)
+        @pl.when(where_ref[base] == mine)
         def _(mine=mine):
             for head in range(PAIR):
                 rows = slice(head * HEAD, (head + 1) * HEAD)
@@ -167,12 +168,12 @@
                 total_ref[head] = top + jnp.log(total)
 
 
-def attend_block(where, starts, buffer, block):
+def attend_block(where, base, starts, buffer, block):
     _, width, length = buffer.shape
     rows = PAIR * HEAD
     heads, blocks = width // HEAD, length // block
     return pl.pallas_call(
-        functools.partial(attend_kernel, blocks, block),
+        functools.partial(attend_kernel, blocks, block, base),
         out_shape=(
             jax.ShapeDtypeStruct((width, block), BF16),
             jax.ShapeDtypeStruct((heads, 1, block), F32),
@@ -181,8 +182,8 @@
             num_scalar_prefetch=1,
             grid=(width // rows,),
             in_specs=[
-                pl.BlockSpec((1, block), lambda h, s: (0, s[0])),
-                pl.BlockSpec((1, rows, block), lambda h, s: (0, h, s[0])),
+                pl.BlockSpec((1, block), lambda h, s: (0, s[base])),
+                pl.BlockSpec((1, rows, block), lambda h, s: (0, h, s[base])),
                 pl.BlockSpec((1, rows, length), lambda h, s: (1, h, 0)),
                 pl.BlockSpec((1, rows, length), lambda h, s: (2, h, 0)),
             ],
@@ -200,7 +201,7 @@
     )(where, starts, buffer, buffer, buffer)
 
 
-def attend_back_kernel(blocks, block, first, last, where_ref, starts_ref, cos_ref, sin_ref, *refs):
+def attend_back_kernel(blocks, block, base, first, last, where_ref, starts_ref, cos_ref, sin_ref, *refs):
     if last:
         all_cos_ref, all_sin_ref, *refs = refs
     q_ref, k_ref, v_ref, grad_ref, total_ref, *refs = refs
@@ -229,7 +230,7 @@
 
     for mine in range(blocks):
 
-        @pl.when(where_ref[0] == mine)
+        @pl.when(where_ref[base] == mine)
         def _(mine=mine):
             for head in range(PAIR):
                 rows = slice(head * HEAD, (head + 1) * HEAD)
@@ -265,7 +266,7 @@
                         key_sum = old_ref[0, rows, columns]
                         value_sum = old_ref[1, rows, columns]
                     if last:
-                        there = at_position(lax.rem(where_ref[2] + blocks - other, blocks))
+                        there = at_position(lax.rem(where_ref[base + 2] + blocks - other, blocks))
                         turned = unrotate(
                             key_sum, all_cos_ref[:, columns], all_sin_ref[:, columns]
                         )
@@ -276,12 +277,12 @@
                         sums_ref[1, rows, columns] = value_sum
                 query_sum = unrotate(query_sum * (HEAD**-0.5), cosine, sine).astype(BF16)
                 if last:
-                    out_ref[0, rows, at_position(where_ref[1])] = query_sum
+                    out_ref[0, rows, at_position(where_ref[base + 1])] = query_sum
                 else:
                     out_ref[rows, :] = query_sum
 
 
-def attend_back_block(where, starts, cosine, sine, buffer, grad, totals, before, last):
+def attend_back_block(where, base, starts, cosine, sine, buffer, grad, totals, before, last):
     _, width, length = buffer.shape
     block = grad.shape[1]
     rows = PAIR * HEAD
@@ -291,20 +292,20 @@
     whole_table = pl.BlockSpec((HALF, length), lambda h, s: (0, 0))
     both = pl.BlockSpec((2, rows, length), lambda h, s: (0, h, 0))
     specs = [
-        pl.BlockSpec((1, block), lambda h, s: (0, s[0])),
-        pl.BlockSpec((HALF, block), lambda h, s: (0, s[0])),
-        pl.BlockSpec((HALF, block), lambda h, s: (0, s[0])),
+        pl.BlockSpec((1, block), lambda h, s: (0, s[base])),
+        pl.BlockSpec((HALF, block), lambda h, s: (0, s[base])),
+        pl.BlockSpec((HALF, block), lambda h, s: (0, s[base])),
     ]
     args = [where, starts, cosine, sine]
     if last:
         specs += [whole_table, whole_table]
         args += [cosine, sine]
     specs += [
-        pl.BlockSpec((1, rows, block), lambda h, s: (0, h, s[0])),
+        pl.BlockSpec((1, rows, block), lambda h, s: (0, h, s[base])),
         pl.BlockSpec((1, rows, length), lambda h, s: (1, h, 0)),
         pl.BlockSpec((1, rows, length), lambda h, s: (2, h, 0)),
         pl.BlockSpec((rows, block), lambda h, s: (h, 0)),
-        pl.BlockSpec((PAIR, 1, block), lambda h, s: (s[1] * groups + h, 0, 0)),
+        pl.BlockSpec((PAIR, 1, block), lambda h, s: (s[base + 3] * groups + h, 0, 0)),
     ]
     args += [buffer, buffer, buffer, grad, totals]
     aliases = {}
@@ -323,9 +324,9 @@
             jax.ShapeDtypeStruct((width, length), BF16),
             jax.ShapeDtypeStruct((2, width, length), F32),
         )
-        out_specs = (pl.BlockSpec((rows, block), lambda h, s: (h, s[1])), both)
+        out_specs = (pl.BlockSpec((rows, block), lambda h, s: (h, s[base + 1])), both)
     return pl.pallas_call(
-        functools.partial(attend_back_kernel, blocks, block, first, last),
+        functools.partial(attend_back_kernel, blocks, block, base, first, last),
         out_shape=out_shape,
         grid_spec=pltpu.PrefetchScalarGridSpec(
             num_scalar_prefetch=1, grid=(groups,), in_specs=specs, out_specs=out_specs
@@ -388,9 +389,6 @@
     def pass_down(values, first, last):
         return pass_on(values, [(i, i - 1) for i in range(first, last + 1)])
 
-    def at_place(table):
-        return jnp.asarray(table, jnp.int32)[place]
-
     def plus(term, moving):
         return (term + moving.astype(F32)).astype(BF16)
 
@@ -401,9 +399,29 @@
         for z in range(n)
     ]
 
-    def where_of(blocks_of_place):
-        mine = at_place(blocks_of_place)
-        return jnp.stack([mine, lax.rem(place + n - mine, n), place]).astype(jnp.int32)
+    taken = [
+        sorted(range(1, n), key=lambda p: (p - 1 if p > z else n - 1 - p, p)) + [0]
+        for z in range(n)
+    ]
+
+    def where_row(z):
+        blocks = [(z - p) % n for p in range(n)] + [(z - p) % n for p in taken[z]]
+        blocks += [z] + [z + d if above else z - d for d, above in arrivals[z]]
+        return [
+            v for b in blocks for v in (b, (z - b) % n, z, taken[z].index((z - b) % n))
+        ]
+
+    where = jnp.asarray([where_row(z) for z in range(n)], jnp.int32)[place]
+
+    def choose(values, ranks):
+        groups = sorted(set(ranks.values()))
+        result = values[groups[0]]
+        for rank in groups[1:]:
+            here = functools.reduce(
+                jnp.logical_or, [place == z for z, r in ranks.items() if r == rank]
+            )
+            result = jnp.where(here, values[rank], result)
+        return result
 
     def gather_weight(shard, axis):
         return lax.all_gather(shard.astype(BF16), "dp", axis=axis, tiled=True)
@@ -419,23 +437,18 @@
     normed_one, unit_one, inverse_one = norm_forward(inputs, norm_gain[0], norm_shift[0])
     starts = run_starts(segment_ids)
     cosine, sine = rotary_tables(starts)
-    wheres = [where_of([(z - p) % n for z in range(n)]) for p in range(n)]
-
-    wheres_back = [where_of(list(range(n)))] + [
-        where_of([z + d if above else z - d for z, (d, above) in enumerate(column)])
-        for column in zip(*arrivals)
-    ]
-
     rows_one = [normed_one.astype(BF16)]
     buffer = None
     for p in range(n):
         if p < n - 1:
             moved = pass_on(rows_one[p])
             rows_one.append(
-                after(moved, cosine, sine, starts, *wheres, *wheres_back) if p == 0 else moved
+                after(moved, cosine, sine, starts, where)
+                if p == 0
+                else moved
             )
         pre = contract(rows_one[p], w_qkv, 1, 1) + qkv_bias.reshape(1, 3 * width)
-        buffer = rope_block(wheres[p], pre, cosine, sine, buffer, width, length)
+        buffer = rope_block(where, 4 * p, pre, cosine, sine, buffer, width, length)
 
     cotangent = after(output_grad, rows_one[n - 1])
     grad_up, grad_down_way = [cotangent], [cotangent]
@@ -443,42 +456,51 @@
         grad_up.append(pass_up(grad_up[hop - 1], hop - 1, n - 2))
         grad_down_way.append(pass_down(grad_down_way[hop - 1], 1, n - hop))
 
-    mixed, totals, parts, lows = [None] * n, [None] * n, [None] * n, [None] * n
-    gate = None
-    for p in [1, *range(n - 1, 1, -1), 0]:
-        where = wheres[p] if gate is None else after(wheres[p], gate)
-        mixed[p], totals[p] = attend_block(where, starts, buffer, block)
-        term = contract(mixed[p], w_proj, 0, 0)
-        parts[p], lows[p] = apart(term, term.astype(BF16)) if p in (1, n - 1) else (term, None)
-        gate = parts[p]
-
-    def scatter_chains(parts, lows, gate=()):
-        up = down = None
-        for step in range(n - 1):
-            term_up, term_down = parts[step + 1], parts[n - 1 - step]
-            send_up = lows[1] if up is None else plus(term_up, up)
-            send_down = lows[n - 1] if down is None else plus(term_down, after(down, send_up))
-            if step == 0 and gate:
-                send_up, send_down = after(send_up, *gate), after(send_down, *gate)
+    mixed, totals, parts = [], [], []
+    for rank in range(n):
+        at = after(where, parts[-1]) if rank else where
+        mixed_one, totals_one = attend_block(at, 4 * (n + rank), starts, buffer, block)
+        mixed.append(mixed_one)
+        totals.append(totals_one)
+        term = contract(mixed_one, w_proj, 0, 0)
+        parts.append(apart(term.astype(BF16) if rank < n - 1 else term)[0])
+
+    def scatter_chains(parts, rank_of, gate=()):
+        first = choose(parts, {0: rank_of(0, 1), n - 1: rank_of(n - 1, n - 1)})
+        up = down = pass_on(after(first, *gate), [(0, 1), (n - 1, n - 2)])
+        for step in range(1, n - 1):
+            up_ranks = {z: rank_of(z, step + 1) for z in range(step + 1)}
+            down_ranks = {z: rank_of(z, n - 1 - step) for z in range(n - 1 - step, n)}
+            send_up = plus(choose(parts, up_ranks).astype(F32), up)
+            send_down = plus(
+                choose(parts, down_ranks).astype(F32), after(down, send_up)
+            )
             up = pass_up(send_up, 0, step)
             down = pass_down(send_down, n - 1 - step, n - 1)
-        return parts[0] + up.astype(F32) + down.astype(F32)
-
-    middle = inputs + scatter_chains(parts, lows)
+        return parts[rank_of(0, 0)].astype(F32) + up.astype(F32) + down.astype(F32)
+
+    middle = inputs + scatter_chains(parts, lambda z, p: taken[z].index(p))
     grad_rows = [output_grad] + [
         jnp.where(place >= p, grad_up[p], grad_down_way[n - p]) for p in range(1, n)
     ]
 
     normed_two, unit_two, inverse_two = norm_forward(middle, norm_gain[1], norm_shift[1])
     rows_two = [normed_two.astype(BF16)]
-    hidden, gate_grads, upper_grads, out_parts, back_parts = [], [], [], [], []
-    out_lows, back_lows = [], []
-    for p in range(n):
-        if p < n - 1:
-            rows_two.append(pass_on(rows_two[p]))
-        gate = jnp.dot(rows_two[p], w_feed[0], preferred_element_type=F32)
-        upper = jnp.dot(rows_two[p], w_feed[1], preferred_element_type=F32)
-        grad_hidden = contract(grad_rows[p], w_down, 1, 1)
+    for hop in range(1, n):
+        rows_two.append(pass_on(rows_two[hop - 1]))
+    halves = [range(n // 2), range(n // 2, n)]
+    rows_half, grad_half, hidden, gate_grads, upper_grads = [], [], [], [], []
+    out_parts, back_parts = [], []
+    for half in halves:
+        rows_here, grads_here = apart(
+            jnp.concatenate([rows_two[p] for p in half], axis=0),
+            jnp.concatenate([grad_rows[p] for p in half], axis=0),
+        )
+        rows_half.append(rows_here)
+        grad_half.append(grads_here)
+        gate = jnp.dot(rows_here, w_feed[0], preferred_element_type=F32)
+        upper = jnp.dot(rows_here, w_feed[1], preferred_element_type=F32)
+        grad_hidden = contract(grads_here, w_down, 1, 1)
         sigma = jax.nn.sigmoid(gate)
         swish = gate * sigma
         hidden_low = (swish * upper).astype(BF16)
@@ -489,38 +511,34 @@
         gate_grads.append(gate_low)
         upper_grads.append(upper_low)
         term = contract(gate_low, w_feed[0], 1, 1) + contract(upper_low, w_feed[1], 1, 1)
-        if p == 1:
-            term, low = apart(term, term.astype(BF16))
-        else:
-            (term,), low = apart(term), None
-        back_parts.append(term)
-        back_lows.append(low)
-        term = jnp.dot(hidden_low, w_down, preferred_element_type=F32)
-        if p in (1, n - 1):
-            term, low = apart(term, term.astype(BF16))
-        else:
-            (term,), low = apart(term), None
-        out_parts.append(term)
-        out_lows.append(low)
+        (term,) = apart(term)
+        back_parts.extend(jnp.split(term, len(half), axis=0))
+        (term,) = apart(jnp.dot(hidden_low, w_down, preferred_element_type=F32).astype(BF16))
+        out_parts.extend(jnp.split(term, len(half), axis=0))
 
     def scatter_sum(grad, axis):
-        return lax.psum_scatter(grad, "dp", scatter_dimension=axis, tiled=True).astype(F32)
+        return lax.psum_scatter(grad, "dp", scatter_dimension=axis, tiled=True)
 
     grad_down = contract(
-        jnp.concatenate(hidden, axis=0), jnp.concatenate(grad_rows, axis=0), 0, 0
+        jnp.concatenate(hidden, axis=0), jnp.concatenate(grad_half, axis=0), 0, 0
     ).astype(BF16)
-    down_sum = scatter_sum(grad_down, 1)
+    down_sum = scatter_sum(grad_down, 1).astype(F32)
     grad_feed = jnp.einsum(
-        "rd,krf->kdf",
-        jnp.concatenate(rows_two, axis=0),
+        "krf,rd->kfd",
         jnp.concatenate(gate_grads + upper_grads, axis=0).reshape(2, length, units),
+        jnp.concatenate(rows_half, axis=0),
         preferred_element_type=F32,
     ).astype(BF16)
-    feed_sum = scatter_sum(grad_feed, 1)
+    feed_sum = with_layout_constraint(
+        scatter_sum(grad_feed, 2).transpose(0, 2, 1), Layout((0, 1, 2))
+    ).astype(F32)
 
     moving = None
     for step in range(1, n):
-        send = back_lows[step] if moving is None else plus(back_parts[step], moving)
+        if moving is None:
+            send = after(back_parts[step].astype(BF16), rows_two[n - 1])
+        else:
+            send = plus(back_parts[step], moving)
         moving = pass_on(send)
     grad_normed_two = back_parts[0] + moving.astype(F32)
 
@@ -538,7 +556,8 @@
     def back_block(slot, last):
         grad_mixed = contract(w_proj, slots[slot], 1, 1).astype(BF16)
         return attend_back_block(
-            wheres_back[slot],
+            where,
+            4 * (2 * n + slot),
             starts,
             cosine,
             sine,
@@ -560,32 +579,28 @@
             chosen = value if chosen is None else jnp.where(here == z, value, chosen)
         slots.append(apart(chosen)[0])
     grad_pre = back_block(n - 1, True)
-    layer_output = middle + scatter_chains(out_parts, out_lows, (ups[1], downs[1]))
+    layer_output = middle + scatter_chains(out_parts, lambda z, p: p, (ups[1], downs[1]))
 
     flat_pre = grad_pre.reshape(3 * width, length)
-    moving = None
+    moving, first_parts = None, [None] * n
     for step in [*range(1, n), 0]:
         term = contract(flat_pre[:, step * block : (step + 1) * block], w_qkv, 0, 0)
-        if step == 0:
-            grad_normed_one = term + moving.astype(F32)
-        else:
-            send = term.astype(BF16) if moving is None else plus(term, moving)
-            moving = pass_on(send)
+        first_parts[step] = apart(term.astype(BF16) if step == 1 else term)[0]
+    for step in range(1, n):
+        send = first_parts[1] if moving is None else plus(first_parts[step], moving)
+        moving = pass_on(send)
+    grad_normed_one = first_parts[0] + moving.astype(F32)
     grad_qkv = contract(flat_pre, jnp.concatenate(rows_one, axis=0), 1, 0).astype(BF16)
     all_mixed = jnp.concatenate(mixed, axis=1)
-    mixed_slots = []
-    for slot in range(n):
-        at = [0] * n if slot == 0 else [
-            (-d if above else d) % n for d, above in (arrivals[z][slot - 1] for z in range(n))
-        ]
-        mixed_slots.append(
-            lax.dynamic_slice_in_dim(all_mixed, at_place(at) * block, block, 1)
-        )
+    mixed_slots = [
+        lax.dynamic_slice_in_dim(all_mixed, where[4 * (2 * n + slot) + 3] * block, block, 1)
+        for slot in range(n)
+    ]
     grad_proj = contract(
         jnp.concatenate(mixed_slots, axis=1), jnp.concatenate(slots, axis=0), 1, 0
     ).astype(BF16)
     grad_both = jnp.concatenate([grad_qkv, grad_proj], axis=0)
-    both_rows = scatter_sum(grad_both, 1)
+    both_rows = scatter_sum(grad_both, 1).astype(F32)
     qkv_sum = both_rows[: 3 * width].reshape(3, width, depth // data_size).transpose(0, 2, 1)
     proj_sum = both_rows[3 * width :]
 

time: 833 us -> 799 us (0.959)
  waiting for transfers between devices: 242 us -> 279 us
  starting transfers between devices: 165 us -> 133 us
  local copies, waits for them, and re-layouts: 45.6 us -> 14.6 us
  matrix products: 183 us -> 170 us
    ppermute x36 -> x34, waiting for transfers between devices: 229 us -> 267 us  [pass_on(): return lax.ppermute(values, 'tensor', pairs)]
    ppermute x36 -> x34, starting transfers between devices: 157 us -> 132 us  [pass_on(): return lax.ppermute(values, 'tensor', pairs)]
    unnamed x251 -> x203, local copies, waits for them, and re-layouts: 33.2 us -> 8.39 us
    concatenate x0 -> x5, other arithmetic: none -> 12.2 us  [the longest x1 4.99 us: per_device(): jnp.concatenate(gate_grads + upper_grads, axis=0).reshape(2, length, units)]
    dot_general x13 -> x7, matrix products: 61.5 us -> 52.3 us  [the longest x2 16.2 us: per_device(): gate = jnp.dot(rows_here, w_feed[0], preferred_element_type=F32)]
    dot_general x31 -> x25, matrix products: 122 us -> 118 us  [contract(): lax.dot_general(left, right, (((left_dim,), (right_dim,)), ((), ())), pre...]
    convert_element_type x10 -> x11, other arithmetic: 18.9 us -> 19.9 us  [plus(): return (term + moving.astype(F32)).astype(BF16)]
  transfers between devices with their start and end apart: 48 -> 46, of which waited for: 22 -> 26; matrix products, arithmetic and copies ran while one was open for 31% -> 29% of each run, Pallas kernels for 9% -> 10%
where the time goes in v1:
time: 799 us; the launch traced here: 794 us
  waiting for transfers between devices  279 us (35%)
  matrix products  170 us (21%)
  starting transfers between devices  133 us (17%)
  other arithmetic  99.9 us (13%)
  Pallas kernels  78.6 us (10%)
  between operations  18.7 us (2%)
  local copies, waits for them, and re-layouts  14.6 us (2%)
    ppermute x34, waiting for transfers between devices, pass_on(): return lax.ppermute(values, 'tensor', pairs)  267 us
    ppermute x34, starting transfers between devices, pass_on(): return lax.ppermute(values, 'tensor', pairs)  132 us
    dot_general x25, matrix products, contract(): lax.dot_general(left, right, (((left_dim,), (right_dim,)), ((), ())), pre...  118 us
    pallas_call x4, Pallas kernels, attend_back_block(): pl.pallas_call(functools.partial(attend_back_kernel, blocks, block, base,...  39.2 us
    pallas_call x4, Pallas kernels, attend_block(): pl.pallas_call(functools.partial(attend_kernel, blocks, block, base), out...  26.9 us
    add x4, other arithmetic, per_device(): shown = change if which < 3 else param_arr + change  21.2 us
    convert_element_type x11, other arithmetic, plus(): return (term + moving.astype(F32)).astype(BF16)  19.9 us
    dot_general x2, matrix products, per_device(): gate = jnp.dot(rows_here, w_feed[0], preferred_element_type=F32)  16.2 us
  transfers between devices with their start and end apart: 46, of which 26 were waited for; matrix products, arithmetic and copies ran while one was open for 29% of the time, Pallas kernels for 10%

profile of v1, /device:TPU:0, one launch (start us, length us, event | category | flops | bytes accessed | tf_op | source)
XLA Modules:
  0.0 794.3 jit_solution(9579932720173367483)
XLA Ops:
  22.6 21.6 %collective-permute-done = bf16[256,2048]{1,0:T(8,128)(2,1)} collective-permute-done((bf16[256,2048]{1,0:T(8,128)(2,1)S(1)}, bf16[256,2048]{1,0:T(8,128)(2,1)}, u32[]{:S(2)}, u32[]{:S(2)}) %collective-permute-start) | collective-permute-done | bytes 1048608 | tf_op jit(solution)/shard_map/ppermute | solution.py:384
  44.3 26.4 %collective-permute-done.1 = bf16[256,2048]{1,0:T(8,128)(2,1)} collective-permute-done((bf16[256,2048]{1,0:T(8,128)(2,1)}, bf16[256,2048]{1,0:T(8,128)(2,1)}, u32[]{:S(2)}, u32[]{:S(2)}) %collective-permute-start.1) | collective-permute-done | bytes 1048608 | tf_op jit(solution)/shard_map/ppermute | solution.py:384
  132.9 9.7 %collective-permute-done.3 = bf16[256,2048]{1,0:T(8,128)(2,1)} collective-permute-done((bf16[256,2048]{1,0:T(8,128)(2,1)}, bf16[256,2048]{1,0:T(8,128)(2,1)}, u32[]{:S(2)}, u32[]{:S(2)}) %collective-permute-start.3) | collective-permute-done | bytes 1048608 | tf_op jit(solution)/shard_map/ppermute | solution.py:384
  180.6 8.6 %collective-permute-start.5 = (bf16[256,2048]{1,0:T(8,128)(2,1)}, bf16[256,2048]{1,0:T(8,128)(2,1)}, u32[]{:S(2)}, u32[]{:S(2)}) collective-permute-start(bf16[256,2048]{1,0:T(8,128)(2,1)} %add_convert_fusion.7), channel_id=1, source_target_pairs={{0,1},{1,2},{2,3},{4,5},{5,6},{6,7},{8,9},{9,10},{10,11},{12,13},{... | collective-permute-start | bytes 3145736 | tf_op jit(solution)/shard_map/ppermute | solution.py:384
  218.7 33.8 %collective-permute-start.8 = (bf16[256,2048]{1,0:T(8,128)(2,1)S(1)}, bf16[256,2048]{1,0:T(8,128)(2,1)}, u32[]{:S(2)}, u32[]{:S(2)}) collective-permute-start(bf16[256,2048]{1,0:T(8,128)(2,1)S(1)} %add_convert_fusion.4), channel_id=1, source_target_pairs={{0,1},{1,2},{2,3},{3,0},{4,5},{5,6},{6,7},{7,4},{8,9},{9,10},{10,1... | collective-permute-start | bytes 3145736 | tf_op jit(solution)/shard_map/ppermute | solution.py:384
  254.6 10.3 %collective-permute-done.8 = bf16[256,2048]{1,0:T(8,128)(2,1)} collective-permute-done((bf16[256,2048]{1,0:T(8,128)(2,1)S(1)}, bf16[256,2048]{1,0:T(8,128)(2,1)}, u32[]{:S(2)}, u32[]{:S(2)}) %collective-permute-start.8) | collective-permute-done | bytes 1048608 | tf_op jit(solution)/shard_map/ppermute | solution.py:384
  264.8 27.5 %collective-permute-start.13 = (bf16[256,2048]{1,0:T(8,128)(2,1)}, bf16[256,2048]{1,0:T(8,128)(2,1)S(1)}, u32[]{:S(2)}, u32[]{:S(2)}) collective-permute-start(bf16[256,2048]{1,0:T(8,128)(2,1)} %collective-permute-done.8), channel_id=1, source_target_pairs={{0,1},{1,2},{2,3},{3,0},{4,5},{5,6},{6,7},{7,4},{8,9},{9,10},{10,1... | collective-permute-start | bytes 3145736 | tf_op jit(solution)/shard_map/ppermute | solution.py:384
  293.7 17.5 %collective-permute-done.12 = bf16[256,2048]{1,0:T(8,128)(2,1)S(1)} collective-permute-done((bf16[256,2048]{1,0:T(8,128)(2,1)}, bf16[256,2048]{1,0:T(8,128)(2,1)S(1)}, u32[]{:S(2)}, u32[]{:S(2)}) %collective-permute-start.12) | collective-permute-done | bytes 1048608 | tf_op jit(solution)/shard_map/ppermute | solution.py:384
  321.4 32.4 %collective-permute-done.14 = bf16[256,2048]{1,0:T(8,128)(2,1)S(1)} collective-permute-done((bf16[256,2048]{1,0:T(8,128)(2,1)S(1)}, bf16[256,2048]{1,0:T(8,128)(2,1)S(1)}, u32[]{:S(2)}, u32[]{:S(2)}) %collective-permute-start.14) | collective-permute-done | bytes 1048608 | tf_op jit(solution)/shard_map/ppermute | solution.py:384
  355.4 8.4 %fusion.23 = f32[512,1408]{1,0:T(8,128)} fusion(bf16[512,2048]{1,0:T(8,128)(2,1)} %pad_maximum_fusion.2, bf16[2,2048,1408]{2,1,0:T(8,128)(2,1)} %all-gather.9.cloned.1.call-done), kind=kOutput, calls=%fused_computation.33 | convolution fusion | flops 2952790016 | bytes 10747904 | tf_op jit(solution)/shard_map/dot_general | solution.py:501
  368.8 9.8 %multiply_convert_fusion.3 = (bf16[512,1408]{1,0:T(8,128)(2,1)}, bf16[512,1408]{1,0:T(8,128)(2,1)}, bf16[512,1408]{1,0:T(8,128)(2,1)}) fusion(f32[512,1408]{1,0:T(8,128)} %fusion.23, f32[512,1408]{1,0:T(8,128)} %fusion.27, bf16[512,2048]{1,0:T(8,128)(2,1)S(1)} %pad_maximum_fusion.3, bf16[1408,2048]{1,0:T(8,128)(2,1)} %all-gather.11.cloned.1.call-done), kind=kOutput, calls=%fused_computation.57 | convolution fusion | flops 2963603456 | bytes 17956864 | tf_op jit(solution)/shard_map/dot_general | solution.py:67
  414.8 15.6 %convolution_convert_fusion = bf16[2,1408,2048]{1,2,0:T(8,128)(2,1)} fusion(bf16[2,1024,1408]{2,1,0:T(8,128)(2,1)S(1)} %bitcast.131, bf16[512,2048]{1,0:T(8,128)(2,1)S(1)} %copy-done.22, bf16[512,2048]{1,0:T(8,128)(2,1)S(1)} %copy-done.20), kind=kOutput, calls=%fused_computation | convolution fusion | flops 11825315840 | bytes 21495808 | tf_op jit(solution)/shard_map/krf,rd->kfd/dot_general | solution.py:526
  454.3 14.7 %collective-permute-done.17 = bf16[256,2048]{1,0:T(8,128)(2,1)S(1)} collective-permute-done((bf16[256,2048]{1,0:T(8,128)(2,1)S(1)}, bf16[256,2048]{1,0:T(8,128)(2,1)S(1)}, u32[]{:S(2)}, u32[]{:S(2)}) %collective-permute-start.17) | collective-permute-done | bytes 1048608 | tf_op jit(solution)/shard_map/ppermute | solution.py:384
  470.5 21.7 %collective-permute-done.18 = bf16[256,2048]{1,0:T(8,128)(2,1)S(1)} collective-permute-done((bf16[256,2048]{1,0:T(8,128)(2,1)S(1)}, bf16[256,2048]{1,0:T(8,128)(2,1)S(1)}, u32[]{:S(2)}, u32[]{:S(2)}) %collective-permute-start.18) | collective-permute-done | bytes 1048608 | tf_op jit(solution)/shard_map/ppermute | solution.py:384
  503.3 8.9 %collective-permute-done.19 = bf16[256,2048]{1,0:T(8,128)(2,1)S(1)} collective-permute-done((bf16[256,2048]{1,0:T(8,128)(2,1)S(1)}, bf16[256,2048]{1,0:T(8,128)(2,1)S(1)}, u32[]{:S(2)}, u32[]{:S(2)}) %collective-permute-start.19) | collective-permute-done | bytes 1048608 | tf_op jit(solution)/shard_map/ppermute | solution.py:384
  554.1 9.7 %attend_back_block.5 = (bf16[512,1024]{1,0:T(8,128)(2,1)}, f32[2,512,1024]{2,1,0:T(8,128)}) custom-call(s32[48]{0:T(128)} %get-tuple-element.74.w.where_ref, s32[1,1024]{1,0:T(1,128)} %reduce_window_max.25.starts_ref, f32[8,1024]{1,0:T(8,128)} %get-tuple-element.161.c.cos_ref.refs_0_, ...), custom_call_target="tpu_custom_call", output_to_operand_aliasing={{0}: (9, {}), {1}: (10, {})} | custom-call | flops 5368709120 | bytes 11272192 | tf_op jit(solution)/shard_map/attend_back_block/pallas_call | solution.py:328
  572.4 10.4 %attend_back_block.6 = (bf16[512,1024]{1,0:T(8,128)(2,1)}, f32[2,512,1024]{2,1,0:T(8,128)}) custom-call(s32[48]{0:T(128)} %get-tuple-element.74.w.where_ref, s32[1,1024]{1,0:T(1,128)} %reduce_window_max.25.starts_ref, f32[8,1024]{1,0:T(8,128)} %get-tuple-element.161.c.cos_ref.refs_0_, ...), custom_call_target="tpu_custom_call", output_to_operand_aliasing={{0}: (9, {}), {1}: (10, {})} | custom-call | flops 5368709120 | bytes 11272192 | tf_op jit(solution)/shard_map/attend_back_block/pallas_call | solution.py:328
  586.7 12.0 %attend_back_block.7 = bf16[3,512,1024]{2,1,0:T(8,128)(2,1)} custom-call(s32[48]{0:T(128)} %get-tuple-element.74.w.where_ref, s32[1,1024]{1,0:T(1,128)} %reduce_window_max.25.starts_ref, f32[8,1024]{1,0:T(8,128)} %get-tuple-element.161.c.cos_ref.refs_0_, f32[8,1024]{1,0:T(8,128)} %get-tuple-element.160.d.sin_ref.refs_1_, ...), custom_call_target="tpu_custom_call" | custom-call | flops 5368709120 | bytes 11272192 | tf_op jit(solution)/shard_map/attend_back_block/pallas_call | solution.py:328
  598.7 11.3 %convolution_convert_fusion.2 = bf16[1536,2048]{1,0:T(8,128)(2,1)} fusion(bf16[1536,1024]{1,0:T(8,128)(2,1)} %bitcast.124, bf16[256,2048]{1,0:T(8,128)(2,1)} %collective-permute-done.2, bf16[256,2048]{1,0:T(8,128)(2,1)} %collective-permute-done.1, bf16[256,2048]{1,0:T(8,128)(2,1)} %collective-permute-done, bf16[256,2048]{1,0:T(8,128)(2,1)S(1)} %copy-done.32), kind=kOutput, calls=%fused_computation.3 | convolution fusion | flops 6462373888 | bytes 13631488 | tf_op jit(solution)/shard_map/dot_general | solution.py:67
  614.9 8.3 %pad_maximum_fusion = bf16[2048,2048]{1,0:T(8,128)(2,1)} fusion(bf16[512,2048]{1,0:T(8,128)(2,1)} %fusion.30, bf16[1536,2048]{1,0:T(8,128)(2,1)} %convolution_convert_fusion.2), kind=kLoop, calls=%fused_computation.1 | loop fusion | flops 16777216 | bytes 16777216 | tf_op jit(solution)/shard_map/concatenate | solution.py:602
  637.5 15.4 %collective-permute-done.23 = bf16[256,2048]{1,0:T(8,128)(2,1)S(1)} collective-permute-done((bf16[256,2048]{1,0:T(8,128)(2,1)S(1)}, bf16[256,2048]{1,0:T(8,128)(2,1)S(1)}, u32[]{:S(2)}, u32[]{:S(2)}) %collective-permute-start.23) | collective-permute-done | bytes 1048608 | tf_op jit(solution)/shard_map/ppermute | solution.py:384
  664.5 10.9 %collective-permute-done.31 = bf16[256,2048]{1,0:T(8,128)(2,1)S(1)} collective-permute-done((bf16[256,2048]{1,0:T(8,128)(2,1)S(1)}, bf16[256,2048]{1,0:T(8,128)(2,1)S(1)}, u32[]{:S(2)}, u32[]{:S(2)}) %collective-permute-start.31) | collective-permute-done | bytes 1048608 | tf_op jit(solution)/shard_map/ppermute | solution.py:384
  682.8 31.0 %collective-permute-done.32 = bf16[256,2048]{1,0:T(8,128)(2,1)S(1)} collective-permute-done((bf16[256,2048]{1,0:T(8,128)(2,1)S(1)}, bf16[256,2048]{1,0:T(8,128)(2,1)S(1)}, u32[]{:S(2)}, u32[]{:S(2)}) %collective-permute-start.32) | collective-permute-done | bytes 1048608 | tf_op jit(solution)/shard_map/ppermute | solution.py:384
  768.5 8.8 %multiply_add_fusion = (f32[2,256,1408]{2,1,0:T(8,128)}, f32[2,256,1408]{2,1,0:T(8,128)}, f32[2,256,1408]{2,1,0:T(8,128)}, f32[2,256,1408]{2,1,0:T(8,128)}) fusion(f32[2,256,1408]{2,1,0:T(8,128)} %param.43, f32[2,256,1408]{2,1,0:T(8,128)} %param.44, f32[2,256,1408]{2,1,0:T(8,128)} %param.45, bf16[2,1408,256]{1,2,0:T(8,128)(2,1)} %reduce-scatter.6.cloned.1.call-done), kind=kLoop, calls=%fused_computation.50 | loop fusion | flops 11534336 | bytes 21626880 | tf_op jit(solution)/shard_map/add | solution.py:639
  (416 shorter events, 390.9 us)
Async XLA Ops:
  7.2 63.8 %all-gather.5.cloned.1.call-start = ((), (), s32[]{:S(2)}) async-start(), calls=%async_computation.3 | async-start | bytes 7077888 | tf_op jit(solution)/shard_map/all_gather | solution.py:427
  9.9 106.7 %all-gather.7.cloned.1.call-start = ((), (), s32[]{:S(2)}) async-start(), calls=%async_computation.4 | async-start | bytes 2359296 | tf_op jit(solution)/shard_map/all_gather | solution.py:427
  10.7 344.7 %all-gather.9.cloned.1.call-start = ((), (), s32[]{:S(2)}) async-start(), calls=%async_computation.5 | async-start | bytes 12976128 | tf_op jit(solution)/shard_map/all_gather | solution.py:427
  14.0 354.8 %all-gather.11.cloned.1.call-start = ((), (), s32[]{:S(2)}) async-start(), calls=%async_computation.6 | async-start | bytes 6488064 | tf_op jit(solution)/shard_map/all_gather | solution.py:427
  123.3 621.3 %reduce-scatter.8.cloned.1.call-start = ((), (), s32[]{:S(2)}) async-start(), calls=%async_computation.9 | async-start | bytes 6488064 | tf_op jit(solution)/shard_map/reduce_scatter | solution.py:520
  156.0 40.5 %collective-permute-start.9 = (bf16[256,2048]{1,0:T(8,128)(2,1)}, bf16[256,2048]{1,0:T(8,128)(2,1)}, u32[]{:S(2)}, u32[]{:S(2)}) collective-permute-start(bf16[256,2048]{1,0:T(8,128)(2,1)} %param.26), channel_id=1, source_target_pairs={{0,1},{1,2},{2,3},{4,5},{5,6},{6,7},{8,9},{9,10},{10,11},{12,13},{... | collective-permute-start | bytes 3145736 | tf_op jit(solution)/shard_map/ppermute | solution.py:384
  158.3 30.9 %collective-permute-start.10 = (bf16[256,2048]{1,0:T(8,128)(2,1)}, bf16[256,2048]{1,0:T(8,128)(2,1)}, u32[]{:S(2)}, u32[]{:S(2)}) collective-permute-start(bf16[256,2048]{1,0:T(8,128)(2,1)} %param.26), channel_id=1, source_target_pairs={{1,0},{2,1},{3,2},{5,4},{6,5},{7,6},{9,8},{10,9},{11,10},{13,12},{... | collective-permute-start | bytes 3145736 | tf_op jit(solution)/shard_map/ppermute | solution.py:384
  179.3 30.8 %collective-permute-start.7 = (bf16[256,2048]{1,0:T(8,128)(2,1)}, bf16[256,2048]{1,0:T(8,128)(2,1)}, u32[]{:S(2)}, u32[]{:S(2)}) collective-permute-start(bf16[256,2048]{1,0:T(8,128)(2,1)} %add_convert_fusion.5), channel_id=1, source_target_pairs={{1,0},{2,1},{3,2},{5,4},{6,5},{7,6},{9,8},{10,9},{11,10},{13,12},{... | collective-permute-start | bytes 3145736 | tf_op jit(solution)/shard_map/ppermute | solution.py:384
  180.6 34.6 %collective-permute-start.5 = (bf16[256,2048]{1,0:T(8,128)(2,1)}, bf16[256,2048]{1,0:T(8,128)(2,1)}, u32[]{:S(2)}, u32[]{:S(2)}) collective-permute-start(bf16[256,2048]{1,0:T(8,128)(2,1)} %add_convert_fusion.7), channel_id=1, source_target_pairs={{0,1},{1,2},{2,3},{4,5},{5,6},{6,7},{8,9},{9,10},{10,11},{12,13},{... | collective-permute-start | bytes 3145736 | tf_op jit(solution)/shard_map/ppermute | solution.py:384
  189.2 63.3 %collective-permute-start.11 = (bf16[256,2048]{1,0:T(8,128)(2,1)}, bf16[256,2048]{1,0:T(8,128)(2,1)}, u32[]{:S(2)}, u32[]{:S(2)}) collective-permute-start(bf16[256,2048]{1,0:T(8,128)(2,1)} %collective-permute-done.10), channel_id=1, source_target_pairs={{1,0},{2,1},{5,4},{6,5},{9,8},{10,9},{13,12},{14,13},{17,16},{18,1... | collective-permute-start | bytes 3145736 | tf_op jit(solution)/shard_map/ppermute | solution.py:384
  196.5 57.3 %collective-permute-start.15 = (bf16[256,2048]{1,0:T(8,128)(2,1)}, bf16[256,2048]{1,0:T(8,128)(2,1)}, u32[]{:S(2)}, u32[]{:S(2)}) collective-permute-start(bf16[256,2048]{1,0:T(8,128)(2,1)} %collective-permute-done.9), channel_id=1, source_target_pairs={{1,2},{2,3},{5,6},{6,7},{9,10},{10,11},{13,14},{14,15},{17,18},{18... | collective-permute-start | bytes 3145736 | tf_op jit(solution)/shard_map/ppermute | solution.py:384
  218.7 46.1 %collective-permute-start.8 = (bf16[256,2048]{1,0:T(8,128)(2,1)S(1)}, bf16[256,2048]{1,0:T(8,128)(2,1)}, u32[]{:S(2)}, u32[]{:S(2)}) collective-permute-start(bf16[256,2048]{1,0:T(8,128)(2,1)S(1)} %add_convert_fusion.4), channel_id=1, source_target_pairs={{0,1},{1,2},{2,3},{3,0},{4,5},{5,6},{6,7},{7,4},{8,9},{9,10},{10,1... | collective-permute-start | bytes 3145736 | tf_op jit(solution)/shard_map/ppermute | solution.py:384
  252.5 58.6 %collective-permute-start.12 = (bf16[256,2048]{1,0:T(8,128)(2,1)}, bf16[256,2048]{1,0:T(8,128)(2,1)S(1)}, u32[]{:S(2)}, u32[]{:S(2)}) collective-permute-start(bf16[256,2048]{1,0:T(8,128)(2,1)} %collective-permute-done.11), channel_id=1, source_target_pairs={{1,0},{5,4},{9,8},{13,12},{17,16},{21,20},{25,24},{29,28}} | collective-permute-start | bytes 3145736 | tf_op jit(solution)/shard_map/ppermute | solution.py:384
  253.8 62.0 %collective-permute-start.16 = (bf16[256,2048]{1,0:T(8,128)(2,1)}, bf16[256,2048]{1,0:T(8,128)(2,1)S(1)}, u32[]{:S(2)}, u32[]{:S(2)}) collective-permute-start(bf16[256,2048]{1,0:T(8,128)(2,1)} %collective-permute-done.15), channel_id=1, source_target_pairs={{2,3},{6,7},{10,11},{14,15},{18,19},{22,23},{26,27},{30,31}} | collective-permute-start | bytes 3145736 | tf_op jit(solution)/shard_map/ppermute | solution.py:384
  264.8 48.6 %collective-permute-start.13 = (bf16[256,2048]{1,0:T(8,128)(2,1)}, bf16[256,2048]{1,0:T(8,128)(2,1)S(1)}, u32[]{:S(2)}, u32[]{:S(2)}) collective-permute-start(bf16[256,2048]{1,0:T(8,128)(2,1)} %collective-permute-done.8), channel_id=1, source_target_pairs={{0,1},{1,2},{2,3},{3,0},{4,5},{5,6},{6,7},{7,4},{8,9},{9,10},{10,1... | collective-permute-start | bytes 3145736 | tf_op jit(solution)/shard_map/ppermute | solution.py:384
  313.4 40.4 %collective-permute-start.14 = (bf16[256,2048]{1,0:T(8,128)(2,1)S(1)}, bf16[256,2048]{1,0:T(8,128)(2,1)S(1)}, u32[]{:S(2)}, u32[]{:S(2)}) collective-permute-start(bf16[256,2048]{1,0:T(8,128)(2,1)S(1)} %collective-permute-done.13), channel_id=1, source_target_pairs={{0,1},{1,2},{2,3},{3,0},{4,5},{5,6},{6,7},{7,4},{8,9},{9,10},{10,1... | collective-permute-start | bytes 3145736 | tf_op jit(solution)/shard_map/ppermute | solution.py:384
  408.5 360.0 %reduce-scatter.6.cloned.1.call-start = ((), (), s32[]{:S(2)}) async-start(), calls=%async_computation.8 | async-start | bytes 12976128 | tf_op jit(solution)/shard_map/reduce_scatter | solution.py:520
  430.5 346.8 %reduce-scatter.4.cloned.1.call-start = ((), (), s32[]{:S(2)}) async-start(), calls=%async_computation.7 | async-start | bytes 9437184 | tf_op jit(solution)/shard_map/reduce_scatter | solution.py:520
  533.8 30.0 %collective-permute-start.27 = (bf16[256,2048]{1,0:T(8,128)(2,1)}, bf16[256,2048]{1,0:T(8,128)(2,1)}, u32[]{:S(2)}, u32[]{:S(2)}) collective-permute-start(bf16[256,2048]{1,0:T(8,128)(2,1)} %collective-permute-done.20), channel_id=1, source_target_pairs={{1,2},{2,3},{5,6},{6,7},{9,10},{10,11},{13,14},{14,15},{17,18},{18... | collective-permute-start | bytes 3145736 | tf_op jit(solution)/shard_map/ppermute | solution.py:384
  545.2 78.1 %collective-permute-start.22 = (bf16[256,2048]{1,0:T(8,128)(2,1)}, bf16[256,2048]{1,0:T(8,128)(2,1)}, u32[]{:S(2)}, u32[]{:S(2)}) collective-permute-start(bf16[256,2048]{1,0:T(8,128)(2,1)} %broadcast_select_fusion.3), channel_id=1, source_target_pairs={{0,1},{3,2},{4,5},{7,6},{8,9},{11,10},{12,13},{15,14},{16,17},{19,... | collective-permute-start | bytes 3145736 | tf_op jit(solution)/shard_map/ppermute | solution.py:384
  635.4 40.0 %collective-permute-start.31 = (bf16[256,2048]{1,0:T(8,128)(2,1)S(1)}, bf16[256,2048]{1,0:T(8,128)(2,1)S(1)}, u32[]{:S(2)}, u32[]{:S(2)}) collective-permute-start(bf16[256,2048]{1,0:T(8,128)(2,1)S(1)} %convolution_convert_fusion.8), channel_id=1, source_target_pairs={{0,1},{1,2},{2,3},{3,0},{4,5},{5,6},{6,7},{7,4},{8,9},{9,10},{10,1... | collective-permute-start | bytes 3145736 | tf_op jit(solution)/shard_map/ppermute | solution.py:384
  656.6 66.7 %collective-permute-start.24 = (bf16[256,2048]{1,0:T(8,128)(2,1)}, bf16[256,2048]{1,0:T(8,128)(2,1)}, u32[]{:S(2)}, u32[]{:S(2)}) collective-permute-start(bf16[256,2048]{1,0:T(8,128)(2,1)} %get-tuple-element.148), channel_id=1, source_target_pairs={{0,1},{1,2},{2,3},{4,5},{5,6},{6,7},{8,9},{9,10},{10,11},{12,13},{... | collective-permute-start | bytes 3145736 | tf_op jit(solution)/shard_map/ppermute | solution.py:384
  675.8 38.0 %collective-permute-start.32 = (bf16[256,2048]{1,0:T(8,128)(2,1)S(1)}, bf16[256,2048]{1,0:T(8,128)(2,1)S(1)}, u32[]{:S(2)}, u32[]{:S(2)}) collective-permute-start(bf16[256,2048]{1,0:T(8,128)(2,1)S(1)} %add_convert_fusion.1), channel_id=1, source_target_pairs={{0,1},{1,2},{2,3},{3,0},{4,5},{5,6},{6,7},{7,4},{8,9},{9,10},{10,1... | collective-permute-start | bytes 3145736 | tf_op jit(solution)/shard_map/ppermute | solution.py:384
  681.5 49.3 %collective-permute-start.26 = (bf16[256,2048]{1,0:T(8,128)(2,1)}, bf16[256,2048]{1,0:T(8,128)(2,1)}, u32[]{:S(2)}, u32[]{:S(2)}) collective-permute-start(bf16[256,2048]{1,0:T(8,128)(2,1)} %add_convert_fusion.2), channel_id=1, source_target_pairs={{1,0},{2,1},{3,2},{5,4},{6,5},{7,6},{9,8},{10,9},{11,10},{13,12},{... | collective-permute-start | bytes 3145736 | tf_op jit(solution)/shard_map/ppermute | solution.py:384
  (118 other events, 1790.5 us)
Sparse Core Ops, SparseCore 0:
  10.5 49.2 all-gather.4
  62.3 28.0 all-gather.6
  92.9 67.5 all-gather.8
  162.8 44.3 all-gather.10
  408.6 58.1 reduce-scatter.7
  470.1 86.9 reduce-scatter.5
  623.4 70.5 reduce-scatter.3

commit v2 on v1

--- a/solution.py
+++ b/solution.py
@@ -437,6 +437,7 @@
     normed_one, unit_one, inverse_one = norm_forward(inputs, norm_gain[0], norm_shift[0])
     starts = run_starts(segment_ids)
     cosine, sine = rotary_tables(starts)
+    (room,) = apart(jnp.zeros((4 * width, depth), BF16))
     rows_one = [normed_one.astype(BF16)]
     buffer = None
     for p in range(n):
@@ -471,7 +472,8 @@
         for step in range(1, n - 1):
             up_ranks = {z: rank_of(z, step + 1) for z in range(step + 1)}
             down_ranks = {z: rank_of(z, n - 1 - step) for z in range(n - 1 - step, n)}
-            send_up = plus(choose(parts, up_ranks).astype(F32), up)
+            ready = up if step == 1 else after(up, send_down)
+            send_up = plus(choose(parts, up_ranks).astype(F32), ready)
             send_down = plus(
                 choose(parts, down_ranks).astype(F32), after(down, send_up)
             )
@@ -511,7 +513,7 @@
         gate_grads.append(gate_low)
         upper_grads.append(upper_low)
         term = contract(gate_low, w_feed[0], 1, 1) + contract(upper_low, w_feed[1], 1, 1)
-        (term,) = apart(term)
+        (term,) = apart(term.astype(BF16))
         back_parts.extend(jnp.split(term, len(half), axis=0))
         (term,) = apart(jnp.dot(hidden_low, w_down, preferred_element_type=F32).astype(BF16))
         out_parts.extend(jnp.split(term, len(half), axis=0))
@@ -523,9 +525,10 @@
         jnp.concatenate(hidden, axis=0), jnp.concatenate(grad_half, axis=0), 0, 0
     ).astype(BF16)
     down_sum = scatter_sum(grad_down, 1).astype(F32)
+    (all_gates,) = apart(jnp.concatenate(gate_grads + upper_grads, axis=0))
     grad_feed = jnp.einsum(
         "krf,rd->kfd",
-        jnp.concatenate(gate_grads + upper_grads, axis=0).reshape(2, length, units),
+        all_gates.reshape(2, length, units),
         jnp.concatenate(rows_half, axis=0),
         preferred_element_type=F32,
     ).astype(BF16)
@@ -536,11 +539,11 @@
     moving = None
     for step in range(1, n):
         if moving is None:
-            send = after(back_parts[step].astype(BF16), rows_two[n - 1])
+            send = after(back_parts[step], rows_two[n - 1])
         else:
-            send = plus(back_parts[step], moving)
+            send = plus(back_parts[step].astype(F32), moving)
         moving = pass_on(send)
-    grad_normed_two = back_parts[0] + moving.astype(F32)
+    grad_normed_two = back_parts[0].astype(F32) + moving.astype(F32)
 
     grad_middle = output_grad.astype(F32) + norm_backward(
         grad_normed_two, unit_two, inverse_two, norm_gain[1]
@@ -599,7 +602,8 @@
     grad_proj = contract(
         jnp.concatenate(mixed_slots, axis=1), jnp.concatenate(slots, axis=0), 1, 0
     ).astype(BF16)
-    grad_both = jnp.concatenate([grad_qkv, grad_proj], axis=0)
+    grad_both = lax.dynamic_update_slice(room, grad_proj, (3 * width, 0))
+    grad_both = lax.dynamic_update_slice(grad_both, grad_qkv, (0, 0))
     both_rows = scatter_sum(grad_both, 1).astype(F32)
     qkv_sum = both_rows[: 3 * width].reshape(3, width, depth // data_size).transpose(0, 2, 1)
     proj_sum = both_rows[3 * width :]
@@ -612,7 +616,8 @@
     def sum_over(values, axis, size):
         step = 1
         while step < size:
-            values = values + lax.ppermute(values, axis, [(i, i ^ step) for i in range(size)])
+            other = lax.ppermute(values, axis, [(i, i ^ step) for i in range(size)])
+            values = values + other
             step *= 2
         return values
 

time: 799 us -> 796 us (level)
  starting transfers between devices: 133 us -> 151 us
  waiting for transfers between devices: 279 us -> 262 us
    ppermute x34, waiting for transfers between devices: 267 us -> 250 us  [pass_on(): return lax.ppermute(values, 'tensor', pairs)]
    ppermute x34, starting transfers between devices: 132 us -> 147 us  [pass_on(): return lax.ppermute(values, 'tensor', pairs)]
    concatenate x2 -> x1, other arithmetic: 13.3 us -> 5.07 us  [per_device(): all_gates, = apart(jnp.concatenate(gate_grads + upper_grads, axis=0))]
    convert_element_type x11 -> x12, other arithmetic: 19.9 us -> 20.8 us  [plus(): return (term + moving.astype(F32)).astype(BF16)]
  transfers between devices with their start and end apart: 46 -> 46, of which waited for: 26 -> 22; matrix products, arithmetic and copies ran while one was open for 29% -> 28% of each run, Pallas kernels for 10% -> 10%
where the time goes in v2:
time: 796 us; the launch traced here: 791 us
  waiting for transfers between devices  262 us (33%)
  matrix products  169 us (21%)
  starting transfers between devices  151 us (19%)
  other arithmetic  92.9 us (12%)
  Pallas kernels  78.5 us (10%)
  local copies, waits for them, and re-layouts  19.1 us (2%)
  between operations  18.6 us (2%)
    ppermute x34, waiting for transfers between devices, pass_on(): return lax.ppermute(values, 'tensor', pairs)  250 us
    ppermute x34, starting transfers between devices, pass_on(): return lax.ppermute(values, 'tensor', pairs)  147 us
    dot_general x25, matrix products, contract(): lax.dot_general(left, right, (((left_dim,), (right_dim,)), ((), ())), pre...  119 us
    pallas_call x4, Pallas kernels, attend_back_block(): pl.pallas_call(functools.partial(attend_back_kernel, blocks, block, base,...  39.1 us
    pallas_call x4, Pallas kernels, attend_block(): pl.pallas_call(functools.partial(attend_kernel, blocks, block, base), out...  26.9 us
    add x4, other arithmetic, per_device(): shown = change if which < 3 else param_arr + change  21.2 us
    convert_element_type x12, other arithmetic, plus(): return (term + moving.astype(F32)).astype(BF16)  20.8 us
    dot_general x2, matrix products, per_device(): gate = jnp.dot(rows_here, w_feed[0], preferred_element_type=F32)  16.2 us
  transfers between devices with their start and end apart: 46, of which 22 were waited for; matrix products, arithmetic and copies ran while one was open for 28% of the time, Pallas kernels for 10%

profile of v2, /device:TPU:0, one launch (start us, length us, event | category | flops | bytes accessed | tf_op | source)
XLA Modules:
  0.0 791.3 jit_solution(14730076959985726117)
XLA Ops:
  22.6 21.6 %collective-permute-done = bf16[256,2048]{1,0:T(8,128)(2,1)} collective-permute-done((bf16[256,2048]{1,0:T(8,128)(2,1)S(1)}, bf16[256,2048]{1,0:T(8,128)(2,1)}, u32[]{:S(2)}, u32[]{:S(2)}) %collective-permute-start) | collective-permute-done | bytes 1048608 | tf_op jit(solution)/shard_map/ppermute | solution.py:384
  44.3 26.4 %collective-permute-done.1 = bf16[256,2048]{1,0:T(8,128)(2,1)} collective-permute-done((bf16[256,2048]{1,0:T(8,128)(2,1)}, bf16[256,2048]{1,0:T(8,128)(2,1)}, u32[]{:S(2)}, u32[]{:S(2)}) %collective-permute-start.1) | collective-permute-done | bytes 1048608 | tf_op jit(solution)/shard_map/ppermute | solution.py:384
  132.8 9.7 %collective-permute-done.3 = bf16[256,2048]{1,0:T(8,128)(2,1)} collective-permute-done((bf16[256,2048]{1,0:T(8,128)(2,1)}, bf16[256,2048]{1,0:T(8,128)(2,1)}, u32[]{:S(2)}, u32[]{:S(2)}) %collective-permute-start.3) | collective-permute-done | bytes 1048608 | tf_op jit(solution)/shard_map/ppermute | solution.py:384
  180.6 8.6 %collective-permute-start.5 = (bf16[256,2048]{1,0:T(8,128)(2,1)}, bf16[256,2048]{1,0:T(8,128)(2,1)}, u32[]{:S(2)}, u32[]{:S(2)}) collective-permute-start(bf16[256,2048]{1,0:T(8,128)(2,1)} %add_convert_fusion.10), channel_id=1, source_target_pairs={{0,1},{1,2},{2,3},{4,5},{5,6},{6,7},{8,9},{9,10},{10,11},{12,13},{... | collective-permute-start | bytes 3145736 | tf_op jit(solution)/shard_map/ppermute | solution.py:384
  218.6 33.9 %collective-permute-start.8 = (bf16[256,2048]{1,0:T(8,128)(2,1)S(1)}, bf16[256,2048]{1,0:T(8,128)(2,1)}, u32[]{:S(2)}, u32[]{:S(2)}) collective-permute-start(bf16[256,2048]{1,0:T(8,128)(2,1)S(1)} %add_convert_fusion.8), channel_id=1, source_target_pairs={{0,1},{1,2},{2,3},{3,0},{4,5},{5,6},{6,7},{7,4},{8,9},{9,10},{10,1... | collective-permute-start | bytes 3145736 | tf_op jit(solution)/shard_map/ppermute | solution.py:384
  254.5 10.3 %collective-permute-done.8 = bf16[256,2048]{1,0:T(8,128)(2,1)} collective-permute-done((bf16[256,2048]{1,0:T(8,128)(2,1)S(1)}, bf16[256,2048]{1,0:T(8,128)(2,1)}, u32[]{:S(2)}, u32[]{:S(2)}) %collective-permute-start.8) | collective-permute-done | bytes 1048608 | tf_op jit(solution)/shard_map/ppermute | solution.py:384
  264.8 27.4 %collective-permute-start.13 = (bf16[256,2048]{1,0:T(8,128)(2,1)}, bf16[256,2048]{1,0:T(8,128)(2,1)S(1)}, u32[]{:S(2)}, u32[]{:S(2)}) collective-permute-start(bf16[256,2048]{1,0:T(8,128)(2,1)} %collective-permute-done.8), channel_id=1, source_target_pairs={{0,1},{1,2},{2,3},{3,0},{4,5},{5,6},{6,7},{7,4},{8,9},{9,10},{10,1... | collective-permute-start | bytes 3145736 | tf_op jit(solution)/shard_map/ppermute | solution.py:384
  293.5 17.5 %collective-permute-done.12 = bf16[256,2048]{1,0:T(8,128)(2,1)S(1)} collective-permute-done((bf16[256,2048]{1,0:T(8,128)(2,1)}, bf16[256,2048]{1,0:T(8,128)(2,1)S(1)}, u32[]{:S(2)}, u32[]{:S(2)}) %collective-permute-start.12) | collective-permute-done | bytes 1048608 | tf_op jit(solution)/shard_map/ppermute | solution.py:384
  321.3 32.2 %collective-permute-done.14 = bf16[256,2048]{1,0:T(8,128)(2,1)S(1)} collective-permute-done((bf16[256,2048]{1,0:T(8,128)(2,1)S(1)}, bf16[256,2048]{1,0:T(8,128)(2,1)S(1)}, u32[]{:S(2)}, u32[]{:S(2)}) %collective-permute-start.14) | collective-permute-done | bytes 1048608 | tf_op jit(solution)/shard_map/ppermute | solution.py:384
  355.1 8.4 %fusion.24 = f32[512,1408]{1,0:T(8,128)} fusion(bf16[512,2048]{1,0:T(8,128)(2,1)} %pad_maximum_fusion.1, bf16[2,2048,1408]{2,1,0:T(8,128)(2,1)} %all-gather.9.cloned.1.call-done), kind=kOutput, calls=%fused_computation.35 | convolution fusion | flops 2952790016 | bytes 10747904 | tf_op jit(solution)/shard_map/dot_general | solution.py:503
  368.6 9.8 %multiply_convert_fusion.3 = (bf16[512,1408]{1,0:T(8,128)(2,1)}, bf16[512,1408]{1,0:T(8,128)(2,1)}, bf16[512,1408]{1,0:T(8,128)(2,1)}) fusion(f32[512,1408]{1,0:T(8,128)} %fusion.24, f32[512,1408]{1,0:T(8,128)} %fusion.28, bf16[512,2048]{1,0:T(8,128)(2,1)S(1)} %pad_maximum_fusion.2, bf16[1408,2048]{1,0:T(8,128)(2,1)} %all-gather.11.cloned.1.call-done), kind=kOutput, calls=%fused_computation.58 | convolution fusion | flops 2963603456 | bytes 17956864 | tf_op jit(solution)/shard_map/dot_general | solution.py:67
  414.7 15.7 %convolution_convert_fusion = bf16[2,1408,2048]{1,2,0:T(8,128)(2,1)} fusion(bf16[2,1024,1408]{2,1,0:T(8,128)(2,1)S(1)} %bitcast.131, bf16[512,2048]{1,0:T(8,128)(2,1)S(1)} %copy-done.24, bf16[512,2048]{1,0:T(8,128)(2,1)S(1)} %copy-done.22), kind=kOutput, calls=%fused_computation | convolution fusion | flops 11825315840 | bytes 21495808 | tf_op jit(solution)/shard_map/krf,rd->kfd/dot_general | solution.py:529
  458.5 11.1 %collective-permute-done.17 = bf16[256,2048]{1,0:T(8,128)(2,1)S(1)} collective-permute-done((bf16[256,2048]{1,0:T(8,128)(2,1)S(1)}, bf16[256,2048]{1,0:T(8,128)(2,1)S(1)}, u32[]{:S(2)}, u32[]{:S(2)}) %collective-permute-start.17) | collective-permute-done | bytes 1048608 | tf_op jit(solution)/shard_map/ppermute | solution.py:384
  471.3 21.6 %collective-permute-done.18 = bf16[256,2048]{1,0:T(8,128)(2,1)S(1)} collective-permute-done((bf16[256,2048]{1,0:T(8,128)(2,1)S(1)}, bf16[256,2048]{1,0:T(8,128)(2,1)S(1)}, u32[]{:S(2)}, u32[]{:S(2)}) %collective-permute-start.18) | collective-permute-done | bytes 1048608 | tf_op jit(solution)/shard_map/ppermute | solution.py:384
  501.0 11.8 %collective-permute-done.19 = bf16[256,2048]{1,0:T(8,128)(2,1)S(1)} collective-permute-done((bf16[256,2048]{1,0:T(8,128)(2,1)S(1)}, bf16[256,2048]{1,0:T(8,128)(2,1)S(1)}, u32[]{:S(2)}, u32[]{:S(2)}) %collective-permute-start.19) | collective-permute-done | bytes 1048608 | tf_op jit(solution)/shard_map/ppermute | solution.py:384
  553.0 9.6 %attend_back_block.5 = (bf16[512,1024]{1,0:T(8,128)(2,1)}, f32[2,512,1024]{2,1,0:T(8,128)}) custom-call(s32[48]{0:T(128)} %get-tuple-element.76.w.where_ref, s32[1,1024]{1,0:T(1,128)} %reduce_window_max.25.starts_ref, f32[8,1024]{1,0:T(8,128)} %get-tuple-element.163.c.cos_ref.refs_0_, ...), custom_call_target="tpu_custom_call", output_to_operand_aliasing={{0}: (9, {}), {1}: (10, {})} | custom-call | flops 5368709120 | bytes 11272192 | tf_op jit(solution)/shard_map/attend_back_block/pallas_call | solution.py:328
  579.3 10.3 %attend_back_block.6 = (bf16[512,1024]{1,0:T(8,128)(2,1)}, f32[2,512,1024]{2,1,0:T(8,128)}) custom-call(s32[48]{0:T(128)} %get-tuple-element.76.w.where_ref, s32[1,1024]{1,0:T(1,128)} %reduce_window_max.25.starts_ref, f32[8,1024]{1,0:T(8,128)} %get-tuple-element.163.c.cos_ref.refs_0_, ...), custom_call_target="tpu_custom_call", output_to_operand_aliasing={{0}: (9, {}), {1}: (10, {})} | custom-call | flops 5368709120 | bytes 11272192 | tf_op jit(solution)/shard_map/attend_back_block/pallas_call | solution.py:328
  593.0 12.0 %attend_back_block.7 = bf16[3,512,1024]{2,1,0:T(8,128)(2,1)} custom-call(s32[48]{0:T(128)} %get-tuple-element.76.w.where_ref, s32[1,1024]{1,0:T(1,128)} %reduce_window_max.25.starts_ref, f32[8,1024]{1,0:T(8,128)} %get-tuple-element.163.c.cos_ref.refs_0_, f32[8,1024]{1,0:T(8,128)} %get-tuple-element.162.d.sin_ref.refs_1_, ...), custom_call_target="tpu_custom_call" | custom-call | flops 5368709120 | bytes 11272192 | tf_op jit(solution)/shard_map/attend_back_block/pallas_call | solution.py:328
  613.2 10.0 %fusion = bf16[2048,2048]{1,0:T(8,128)(2,1)} fusion(bf16[2048,2048]{1,0:T(8,128)(2,1)} %fusion.32, bf16[1536,1024]{1,0:T(8,128)(2,1)S(1)} %bitcast.125, bf16[256,2048]{1,0:T(8,128)(2,1)} %collective-permute-done.2, bf16[256,2048]{1,0:T(8,128)(2,1)} %collective-permute-done.1, bf16[256,2048]{1,0:T(8,128)(2,1)} %collective-permute-done, ...), kind=kOutput, calls=%fused_computation.3 | convolution fusion | flops 6462373888 | bytes 13631488 | tf_op jit(solution)/shard_map/dot_general | solution.py:67
  645.8 24.8 %collective-permute-done.31 = bf16[256,2048]{1,0:T(8,128)(2,1)S(1)} collective-permute-done((bf16[256,2048]{1,0:T(8,128)(2,1)S(1)}, bf16[256,2048]{1,0:T(8,128)(2,1)S(1)}, u32[]{:S(2)}, u32[]{:S(2)}) %collective-permute-start.31) | collective-permute-done | bytes 1048608 | tf_op jit(solution)/shard_map/ppermute | solution.py:384
  670.9 17.3 %collective-permute-start.32 = (bf16[256,2048]{1,0:T(8,128)(2,1)S(1)}, bf16[256,2048]{1,0:T(8,128)(2,1)S(1)}, u32[]{:S(2)}, u32[]{:S(2)}) collective-permute-start(bf16[256,2048]{1,0:T(8,128)(2,1)S(1)} %add_convert_fusion.3), channel_id=1, source_target_pairs={{0,1},{1,2},{2,3},{3,0},{4,5},{5,6},{6,7},{7,4},{8,9},{9,10},{10,1... | collective-permute-start | bytes 3145736 | tf_op jit(solution)/shard_map/ppermute | solution.py:384
  692.7 14.7 %collective-permute-done.32 = bf16[256,2048]{1,0:T(8,128)(2,1)S(1)} collective-permute-done((bf16[256,2048]{1,0:T(8,128)(2,1)S(1)}, bf16[256,2048]{1,0:T(8,128)(2,1)S(1)}, u32[]{:S(2)}, u32[]{:S(2)}) %collective-permute-start.32) | collective-permute-done | bytes 1048608 | tf_op jit(solution)/shard_map/ppermute | solution.py:384
  715.1 17.5 %collective-permute-done.26 = bf16[256,2048]{1,0:T(8,128)(2,1)} collective-permute-done((bf16[256,2048]{1,0:T(8,128)(2,1)}, bf16[256,2048]{1,0:T(8,128)(2,1)}, u32[]{:S(2)}, u32[]{:S(2)}) %collective-permute-start.26) | collective-permute-done | bytes 1048608 | tf_op jit(solution)/shard_map/ppermute | solution.py:384
  765.4 8.8 %multiply_add_fusion = (f32[2,256,1408]{2,1,0:T(8,128)}, f32[2,256,1408]{2,1,0:T(8,128)}, f32[2,256,1408]{2,1,0:T(8,128)}, f32[2,256,1408]{2,1,0:T(8,128)}) fusion(f32[2,256,1408]{2,1,0:T(8,128)} %param.43, f32[2,256,1408]{2,1,0:T(8,128)} %param.44, f32[2,256,1408]{2,1,0:T(8,128)} %param.45, bf16[2,1408,256]{1,2,0:T(8,128)(2,1)} %reduce-scatter.6.cloned.1.call-done), kind=kLoop, calls=%fused_computation.51 | loop fusion | flops 11534336 | bytes 21626880 | tf_op jit(solution)/shard_map/add | solution.py:644
  (425 shorter events, 381.4 us)
Async XLA Ops:
  7.2 63.8 %all-gather.5.cloned.1.call-start = ((), (), s32[]{:S(2)}) async-start(), calls=%async_computation.3 | async-start | bytes 7077888 | tf_op jit(solution)/shard_map/all_gather | solution.py:427
  9.9 106.7 %all-gather.7.cloned.1.call-start = ((), (), s32[]{:S(2)}) async-start(), calls=%async_computation.4 | async-start | bytes 2359296 | tf_op jit(solution)/shard_map/all_gather | solution.py:427
  10.7 344.4 %all-gather.9.cloned.1.call-start = ((), (), s32[]{:S(2)}) async-start(), calls=%async_computation.5 | async-start | bytes 12976128 | tf_op jit(solution)/shard_map/all_gather | solution.py:427
  14.0 354.6 %all-gather.11.cloned.1.call-start = ((), (), s32[]{:S(2)}) async-start(), calls=%async_computation.6 | async-start | bytes 6488064 | tf_op jit(solution)/shard_map/all_gather | solution.py:427
  123.3 615.6 %reduce-scatter.8.cloned.1.call-start = ((), (), s32[]{:S(2)}) async-start(), calls=%async_computation.9 | async-start | bytes 6488064 | tf_op jit(solution)/shard_map/reduce_scatter | solution.py:522
  156.0 40.5 %collective-permute-start.9 = (bf16[256,2048]{1,0:T(8,128)(2,1)}, bf16[256,2048]{1,0:T(8,128)(2,1)}, u32[]{:S(2)}, u32[]{:S(2)}) collective-permute-start(bf16[256,2048]{1,0:T(8,128)(2,1)} %param.26), channel_id=1, source_target_pairs={{0,1},{1,2},{2,3},{4,5},{5,6},{6,7},{8,9},{9,10},{10,11},{12,13},{... | collective-permute-start | bytes 3145736 | tf_op jit(solution)/shard_map/ppermute | solution.py:384
  158.3 30.9 %collective-permute-start.10 = (bf16[256,2048]{1,0:T(8,128)(2,1)}, bf16[256,2048]{1,0:T(8,128)(2,1)}, u32[]{:S(2)}, u32[]{:S(2)}) collective-permute-start(bf16[256,2048]{1,0:T(8,128)(2,1)} %param.26), channel_id=1, source_target_pairs={{1,0},{2,1},{3,2},{5,4},{6,5},{7,6},{9,8},{10,9},{11,10},{13,12},{... | collective-permute-start | bytes 3145736 | tf_op jit(solution)/shard_map/ppermute | solution.py:384
  179.3 30.9 %collective-permute-start.7 = (bf16[256,2048]{1,0:T(8,128)(2,1)}, bf16[256,2048]{1,0:T(8,128)(2,1)}, u32[]{:S(2)}, u32[]{:S(2)}) collective-permute-start(bf16[256,2048]{1,0:T(8,128)(2,1)} %add_convert_fusion.9), channel_id=1, source_target_pairs={{1,0},{2,1},{3,2},{5,4},{6,5},{7,6},{9,8},{10,9},{11,10},{13,12},{... | collective-permute-start | bytes 3145736 | tf_op jit(solution)/shard_map/ppermute | solution.py:384
  180.6 34.6 %collective-permute-start.5 = (bf16[256,2048]{1,0:T(8,128)(2,1)}, bf16[256,2048]{1,0:T(8,128)(2,1)}, u32[]{:S(2)}, u32[]{:S(2)}) collective-permute-start(bf16[256,2048]{1,0:T(8,128)(2,1)} %add_convert_fusion.10), channel_id=1, source_target_pairs={{0,1},{1,2},{2,3},{4,5},{5,6},{6,7},{8,9},{9,10},{10,11},{12,13},{... | collective-permute-start | bytes 3145736 | tf_op jit(solution)/shard_map/ppermute | solution.py:384
  189.1 63.3 %collective-permute-start.11 = (bf16[256,2048]{1,0:T(8,128)(2,1)}, bf16[256,2048]{1,0:T(8,128)(2,1)}, u32[]{:S(2)}, u32[]{:S(2)}) collective-permute-start(bf16[256,2048]{1,0:T(8,128)(2,1)} %collective-permute-done.10), channel_id=1, source_target_pairs={{1,0},{2,1},{5,4},{6,5},{9,8},{10,9},{13,12},{14,13},{17,16},{18,1... | collective-permute-start | bytes 3145736 | tf_op jit(solution)/shard_map/ppermute | solution.py:384
  196.4 57.4 %collective-permute-start.15 = (bf16[256,2048]{1,0:T(8,128)(2,1)}, bf16[256,2048]{1,0:T(8,128)(2,1)}, u32[]{:S(2)}, u32[]{:S(2)}) collective-permute-start(bf16[256,2048]{1,0:T(8,128)(2,1)} %collective-permute-done.9), channel_id=1, source_target_pairs={{1,2},{2,3},{5,6},{6,7},{9,10},{10,11},{13,14},{14,15},{17,18},{18... | collective-permute-start | bytes 3145736 | tf_op jit(solution)/shard_map/ppermute | solution.py:384
  218.6 46.2 %collective-permute-start.8 = (bf16[256,2048]{1,0:T(8,128)(2,1)S(1)}, bf16[256,2048]{1,0:T(8,128)(2,1)}, u32[]{:S(2)}, u32[]{:S(2)}) collective-permute-start(bf16[256,2048]{1,0:T(8,128)(2,1)S(1)} %add_convert_fusion.8), channel_id=1, source_target_pairs={{0,1},{1,2},{2,3},{3,0},{4,5},{5,6},{6,7},{7,4},{8,9},{9,10},{10,1... | collective-permute-start | bytes 3145736 | tf_op jit(solution)/shard_map/ppermute | solution.py:384
  252.5 58.5 %collective-permute-start.12 = (bf16[256,2048]{1,0:T(8,128)(2,1)}, bf16[256,2048]{1,0:T(8,128)(2,1)S(1)}, u32[]{:S(2)}, u32[]{:S(2)}) collective-permute-start(bf16[256,2048]{1,0:T(8,128)(2,1)} %collective-permute-done.11), channel_id=1, source_target_pairs={{1,0},{5,4},{9,8},{13,12},{17,16},{21,20},{25,24},{29,28}} | collective-permute-start | bytes 3145736 | tf_op jit(solution)/shard_map/ppermute | solution.py:384
  253.8 61.9 %collective-permute-start.16 = (bf16[256,2048]{1,0:T(8,128)(2,1)}, bf16[256,2048]{1,0:T(8,128)(2,1)S(1)}, u32[]{:S(2)}, u32[]{:S(2)}) collective-permute-start(bf16[256,2048]{1,0:T(8,128)(2,1)} %collective-permute-done.15), channel_id=1, source_target_pairs={{2,3},{6,7},{10,11},{14,15},{18,19},{22,23},{26,27},{30,31}} | collective-permute-start | bytes 3145736 | tf_op jit(solution)/shard_map/ppermute | solution.py:384
  264.8 48.5 %collective-permute-start.13 = (bf16[256,2048]{1,0:T(8,128)(2,1)}, bf16[256,2048]{1,0:T(8,128)(2,1)S(1)}, u32[]{:S(2)}, u32[]{:S(2)}) collective-permute-start(bf16[256,2048]{1,0:T(8,128)(2,1)} %collective-permute-done.8), channel_id=1, source_target_pairs={{0,1},{1,2},{2,3},{3,0},{4,5},{5,6},{6,7},{7,4},{8,9},{9,10},{10,1... | collective-permute-start | bytes 3145736 | tf_op jit(solution)/shard_map/ppermute | solution.py:384
  313.3 40.3 %collective-permute-start.14 = (bf16[256,2048]{1,0:T(8,128)(2,1)S(1)}, bf16[256,2048]{1,0:T(8,128)(2,1)S(1)}, u32[]{:S(2)}, u32[]{:S(2)}) collective-permute-start(bf16[256,2048]{1,0:T(8,128)(2,1)S(1)} %collective-permute-done.13), channel_id=1, source_target_pairs={{0,1},{1,2},{2,3},{3,0},{4,5},{5,6},{6,7},{7,4},{8,9},{9,10},{10,1... | collective-permute-start | bytes 3145736 | tf_op jit(solution)/shard_map/ppermute | solution.py:384
  408.3 357.1 %reduce-scatter.6.cloned.1.call-start = ((), (), s32[]{:S(2)}) async-start(), calls=%async_computation.8 | async-start | bytes 12976128 | tf_op jit(solution)/shard_map/reduce_scatter | solution.py:522
  430.5 343.8 %reduce-scatter.4.cloned.1.call-start = ((), (), s32[]{:S(2)}) async-start(), calls=%async_computation.7 | async-start | bytes 9437184 | tf_op jit(solution)/shard_map/reduce_scatter | solution.py:522
  533.5 29.1 %collective-permute-start.27 = (bf16[256,2048]{1,0:T(8,128)(2,1)}, bf16[256,2048]{1,0:T(8,128)(2,1)}, u32[]{:S(2)}, u32[]{:S(2)}) collective-permute-start(bf16[256,2048]{1,0:T(8,128)(2,1)} %collective-permute-done.20), channel_id=1, source_target_pairs={{1,2},{2,3},{5,6},{6,7},{9,10},{10,11},{13,14},{14,15},{17,18},{18... | collective-permute-start | bytes 3145736 | tf_op jit(solution)/shard_map/ppermute | solution.py:384
  569.7 56.1 %collective-permute-start.23 = (bf16[256,2048]{1,0:T(8,128)(2,1)}, bf16[256,2048]{1,0:T(8,128)(2,1)}, u32[]{:S(2)}, u32[]{:S(2)}) collective-permute-start(bf16[256,2048]{1,0:T(8,128)(2,1)} %fusion.55), channel_id=1, source_target_pairs={{0,1},{1,2},{4,5},{5,6},{8,9},{9,10},{12,13},{13,14},{16,17},{17,1... | collective-permute-start | bytes 3145736 | tf_op jit(solution)/shard_map/ppermute | solution.py:384
  631.6 39.0 %collective-permute-start.31 = (bf16[256,2048]{1,0:T(8,128)(2,1)S(1)}, bf16[256,2048]{1,0:T(8,128)(2,1)S(1)}, u32[]{:S(2)}, u32[]{:S(2)}) collective-permute-start(bf16[256,2048]{1,0:T(8,128)(2,1)S(1)} %convolution_convert_fusion.8), channel_id=1, source_target_pairs={{0,1},{1,2},{2,3},{3,0},{4,5},{5,6},{6,7},{7,4},{8,9},{9,10},{10,1... | collective-permute-start | bytes 3145736 | tf_op jit(solution)/shard_map/ppermute | solution.py:384
  638.3 94.3 %collective-permute-start.24 = (bf16[256,2048]{1,0:T(8,128)(2,1)}, bf16[256,2048]{1,0:T(8,128)(2,1)}, u32[]{:S(2)}, u32[]{:S(2)}) collective-permute-start(bf16[256,2048]{1,0:T(8,128)(2,1)} %add_convert_fusion.5), channel_id=1, source_target_pairs={{0,1},{1,2},{2,3},{4,5},{5,6},{6,7},{8,9},{9,10},{10,11},{12,13},{... | collective-permute-start | bytes 3145736 | tf_op jit(solution)/shard_map/ppermute | solution.py:384
  670.9 36.6 %collective-permute-start.32 = (bf16[256,2048]{1,0:T(8,128)(2,1)S(1)}, bf16[256,2048]{1,0:T(8,128)(2,1)S(1)}, u32[]{:S(2)}, u32[]{:S(2)}) collective-permute-start(bf16[256,2048]{1,0:T(8,128)(2,1)S(1)} %add_convert_fusion.3), channel_id=1, source_target_pairs={{0,1},{1,2},{2,3},{3,0},{4,5},{5,6},{6,7},{7,4},{8,9},{9,10},{10,1... | collective-permute-start | bytes 3145736 | tf_op jit(solution)/shard_map/ppermute | solution.py:384
  689.6 43.0 %collective-permute-start.26 = (bf16[256,2048]{1,0:T(8,128)(2,1)}, bf16[256,2048]{1,0:T(8,128)(2,1)}, u32[]{:S(2)}, u32[]{:S(2)}) collective-permute-start(bf16[256,2048]{1,0:T(8,128)(2,1)} %add_convert_fusion.4), channel_id=1, source_target_pairs={{1,0},{2,1},{3,2},{5,4},{6,5},{7,6},{9,8},{10,9},{11,10},{13,12},{... | collective-permute-start | bytes 3145736 | tf_op jit(solution)/shard_map/ppermute | solution.py:384
  (122 other events, 1834.3 us)
Sparse Core Ops, SparseCore 0:
  10.5 49.2 all-gather.4
  62.3 28.0 all-gather.6
  92.9 67.6 all-gather.8
  162.9 44.2 all-gather.10
  408.4 58.1 reduce-scatter.7
  469.9 86.9 reduce-scatter.5
  623.3 69.8 reduce-scatter.3
